TPU v7x, 512 devices: a whole 4x8x8 slice. The times are simulated.
512 devices in a mesh: fibre: 16 (over y, core), col: 32 (over x, z).
Axes of the slice: x: 4, y: 8, z: 8, core: 2. Of those that a mesh axis runs over, the one named last changes fastest.
Arguments:
- field: float32 [640, 160, 4096], P('fibre', None, 'col'), may hold values from -180 to 180, as said below
- start: float32 [640, 160], replicated, may hold values from -6 to 6
Outputs:
- basis: float32 [640, 160], replicated
- core: float32 [160, 160, 4096], P(None, 'fibre', 'col')
Inputs may be any that keep to these rules, and one draw needn't show every extreme that they name: `field`: entries are finite real values.
All inputs are finite; a program needn't handle non-finite values.
Results may differ from a plain program's by a relative error of at most 0.00016.
Values sent between devices are 32-bit elements; how exact they have to be, the bound alone decides.
No kernel may reach another device: no remote copies, remote signals or barrier semaphores. Data moves between devices by JAX's collectives and lax.ppermute only.
A program may use at most 64 MiB of HBM per device.

v0:
```python
import jax
import jax.numpy as jnp
from jax import lax
from jax.sharding import PartitionSpec as P

ITERS = 2


def subspace(gram, start):
    block = start
    for turn in range(ITERS):
        image = jnp.dot(
            gram, block, precision=lax.Precision.HIGHEST, preferred_element_type=jnp.float32
        )
        small = jnp.dot(
            image.T, image, precision=lax.Precision.HIGHEST, preferred_element_type=jnp.float32
        )
        factor = jnp.linalg.cholesky(small)
        block = lax.linalg.triangular_solve(
            factor, image, left_side=False, lower=True, transpose_a=True
        )
    return block


def shards(field, start):
    regrouped = lax.all_to_all(field, "fibre", split_axis=1, concat_axis=0, tiled=True)
    rows_all = regrouped.shape[0]
    unfolded = regrouped.reshape(rows_all, -1)
    local_gram = jnp.dot(
        unfolded, unfolded.T, precision=lax.Precision.HIGHEST, preferred_element_type=jnp.float32
    )
    gram = lax.psum(local_gram, ("fibre", "col"))
    basis = subspace(gram, start)
    core = jnp.dot(
        basis.T, unfolded, precision=lax.Precision.HIGHEST, preferred_element_type=jnp.float32
    )
    return (basis, core.reshape(basis.shape[1], regrouped.shape[1], regrouped.shape[2]))


def solution(mesh):
    in_specs = (P("fibre", None, "col"), P())
    out_specs = (P(), P(None, "fibre", "col"))
    return jax.shard_map(shards, mesh=mesh, in_specs=in_specs, out_specs=out_specs, check_vma=False)
```

profile of v0, /device:TPU:1, one launch (start us, length us, event | category | flops | bytes accessed | tf_op | source)
XLA Modules:
  0.0 504.5 jit_solution(5928552759673224963)
XLA Ops:
  7.2 0.0 copy-start
  7.2 0.0 all-reduce.5.cloned.1.call-start
  7.2 3.9 copy.7
  11.1 86.0 %all_to_all.15 = f32[40,160,128]{2,0,1:T(8,128)S(1)} all-to-all(f32[40,160,128]{2,0,1:T(8,128)S(1)} %copy.7), channel_id=1, replica_groups=mesh['fibre'=16,'col'=32] {'fibre'}, dimensions={1} | all-to-all | bytes 6553600 | tf_op jit(solution)/shard_map/all_to_all | solution.py:26
  97.1 0.8 copy.8
  97.9 0.0 copy-start.1
  97.9 2.3 copy-done.1
  100.2 10.5 %fusion = f32[640,640]{1,0:T(8,128)} fusion(f32[80,8,10,128]{3,2,1,0:T(8,128)S(1)} %bitcast.77), kind=kOutput, calls=%fused_computation.1 | convolution fusion | flops 6291456000 | bytes 4915200 | tf_op jit(solution)/shard_map/dot_general | solution.py:29
  110.8 0.0 all-reduce.5.cloned.1.call-update
  110.9 5.8 %copy.18 = f32[80,8,10,128]{3,1,2,0:T(8,128)} copy(f32[80,8,10,128]{3,2,1,0:T(8,128)} %bitcast.78) | data formatting | bytes 6553600
  116.6 4.8 copy.11
  121.4 265.6 %all-reduce.5.cloned.1.call-done = f32[640,640]{1,0:T(8,128)} async-done(((f32[640,640]{1,0:T(8,128)}), f32[640,640]{1,0:T(8,128)}) %all-reduce.5.cloned.1.call-update) | async-done | bytes 1638416 | tf_op jit(solution)/shard_map/psum | solution.py:32
  387.0 0.0 copy-done
  387.0 0.0 copy-start.2
  387.0 3.3 fusion.30
  390.3 0.6 fusion.31
  390.9 0.1 copy.9
  391.0 11.7 %cholesky.136 = f32[128,128]{1,0:T(8,128)S(1)} custom-call(f32[128,128]{1,0:T(8,128)S(1)} %cholesky.208), custom_call_target="Cholesky" | custom-call | tf_op jit(solution)/shard_map/jit(cholesky)/cholesky | solution.py:18
  402.8 9.8 %custom-call.13 = f32[1,128,128]{1,2,0:T(8,128)S(1)} custom-call(f32[1,128,128]{2,1,0:T(8,128)S(1)} %get-tuple-element.33), custom_call_target="InvertDiagBlocksLowerTriangular" | custom-call | tf_op jit(solution)/shard_map/jit(cholesky)/cholesky | solution.py:18
  412.6 0.2 constant_dynamic-update-slice_fusion.3
  412.8 0.2 convolution_subtract_fusion.3
  413.0 2.9 cholesky.156
  415.9 0.6 compare_reduce_fusion.2
  416.6 0.6 compare_reduce_fusion.3
  418.5 0.1 fusion.16
  418.6 20.1 %custom-call.14 = f32[2,128,128]{1,2,0:T(8,128)S(1)} custom-call(f32[2,128,128]{2,1,0:T(8,128)S(1)} %pad_maximum_fusion.1), custom_call_target="InvertDiagBlocksLowerTriangular" | custom-call | tf_op jit(solution)/shard_map/triangular_solve/custom-call.0 | solution.py:19
  438.7 0.5 fusion.11
  439.2 0.3 convolution_subtract_fusion.1
  439.5 0.3 fusion.26
  439.8 0.0 copy-done.2
  439.8 1.8 fusion.3
  441.6 0.6 fusion.32
  442.2 0.1 copy.10
  442.3 11.7 %cholesky.174 = f32[128,128]{1,0:T(8,128)S(1)} custom-call(f32[128,128]{1,0:T(8,128)S(1)} %cholesky.211), custom_call_target="Cholesky" | custom-call | tf_op jit(solution)/shard_map/jit(cholesky)/cholesky | solution.py:18
  454.1 9.8 %custom-call.15 = f32[1,128,128]{1,2,0:T(8,128)S(1)} custom-call(f32[1,128,128]{2,1,0:T(8,128)S(1)} %get-tuple-element.31), custom_call_target="InvertDiagBlocksLowerTriangular" | custom-call | tf_op jit(solution)/shard_map/jit(cholesky)/cholesky | solution.py:18
  463.9 0.2 constant_dynamic-update-slice_fusion.1
  464.1 0.2 convolution_subtract_fusion.2
  464.2 2.9 cholesky.194
  467.2 0.6 compare_reduce_fusion
  467.8 0.6 compare_reduce_fusion.1
  469.8 0.1 fusion.15
  469.9 19.8 %custom-call.16 = f32[2,128,128]{1,2,0:T(8,128)S(1)} custom-call(f32[2,128,128]{2,1,0:T(8,128)S(1)} %pad_maximum_fusion.2), custom_call_target="InvertDiagBlocksLowerTriangular" | custom-call | tf_op jit(solution)/shard_map/triangular_solve/custom-call.0 | solution.py:19
  489.8 0.5 fusion.9
  490.3 0.3 convolution_subtract_fusion
  490.6 0.3 fusion.23
  490.9 0.0 copy-start.3
  490.9 6.6 %fusion.7 = f32[160,10,128]{2,0,1:T(8,128)} fusion(f32[10,128,640]{2,1,0:T(8,128)} %bitcast.79, f32[640,160]{0,1:T(8,128)S(1)} %pad_maximum_fusion), kind=kOutput, calls=%fused_computation.13 | convolution fusion | flops 1572864000 | bytes 4505600 | tf_op jit(solution)/shard_map/dot_general | solution.py:34
  497.5 0.0 copy-done.3
  (20 shorter events, 0.3 us)
Async XLA Ops:
  7.2 379.8 %copy-start = (f32[640,160]{0,1:T(8,128)S(1)}, f32[640,160]{0,1:T(8,128)}, u32[]{:S(2)}) copy-start(f32[640,160]{0,1:T(8,128)} %param.6) | copy-start | bytes 1228804
  7.2 379.8 %all-reduce.5.cloned.1.call-start = ((), (), s32[]{:S(2)}) async-start(), calls=%async_computation.1 | async-start | bytes 3276800 | tf_op jit(solution)/shard_map/psum | solution.py:32
  97.9 2.3 copy-start.1
  387.0 52.8 %copy-start.2 = (f32[640,640]{1,0:T(8,128)S(1)}, f32[640,640]{1,0:T(8,128)}, u32[]{:S(2)}) copy-start(f32[640,640]{1,0:T(8,128)} %all-reduce.5.cloned.1.call-done) | copy-start | bytes 4915204
  490.9 6.6 %copy-start.3 = (f32[640,160]{0,1:T(8,128)}, f32[640,160]{0,1:T(8,128)S(1)}, u32[]{:S(2)}) copy-start(f32[640,160]{0,1:T(8,128)S(1)} %pad_maximum_fusion) | copy-start | bytes 1228804
Sparse Core Ops, SparseCore 0:
  110.9 275.9 all-reduce.4
where the time goes:
time: 508 us; the launch traced here: 505 us
  waiting for transfers between devices  266 us (52%)
  other arithmetic  91.8 us (18%)
  blocking collectives  86 us (17%)
  matrix products  26.1 us (5%)
  local copies, waits for them, and re-layouts  17.8 us (4%)
  between operations  17.1 us (3%)
    psum x1, waiting for transfers between devices, shards(): gram = lax.psum(local_gram, ('fibre', 'col'))  266 us
    all_to_all x1, blocking collectives, shards(): lax.all_to_all(field, 'fibre', split_axis=1, concat_axis=0, tiled=True)  86 us
    another operation x14, other arithmetic, subspace(): factor = jnp.linalg.cholesky(small)  51.6 us
    another operation x11, other arithmetic, subspace(): lax.linalg.triangular_solve(factor, image, left_side=False, lower=True, t...  40.2 us
    unnamed x10, local copies, waits for them, and re-layouts  12 us
    dot_general x1, matrix products, shards(): jnp.dot(unfolded, unfolded.T, precision=lax.Precision.HIGHEST, preferred_...  10.5 us
  transfers between devices with their start and end apart: 1, of which 1 were waited for; matrix products, arithmetic and copies ran while one was open for 2% of the time, Pallas kernels for 0%

commit v1 on v0

v1 whole, which is shorter than its diff:
```python
import functools
import jax, jax.numpy as jnp
from jax import lax
from jax.experimental import pallas as pl
from jax.experimental.pallas import tpu as pltpu
from jax.sharding import PartitionSpec as P
HI=lax.Precision.HIGHEST
f32=jnp.float32
NT=(((1,),(1,)),((),())); NN=(((1,),(0,)),((),())); TN=(((0,),(0,)),((),()))
def dot(a,b,d=NN,prec=HI): return lax.dot_general(a,b,d,precision=prec,preferred_element_type=f32)
NB=32
def inv_diag1(X,nb=NB):
    row=lax.broadcasted_iota(jnp.int32,(nb,1),0)
    for j in range(nb-1):
        t=(j+1)//8*8
        r=X[j:j+1,:]; c=X[t:,j:j+1]; p=X[j:j+1,j:j+1]
        m=jnp.where(row[t:]>j,c*(1.0/p),0.0)
        Y=X[t:]-m*r
        X=jnp.concatenate([X[:t],Y]) if t else Y
    lane=lax.broadcasted_iota(jnp.int32,(nb,128),1)
    rw=lax.broadcasted_iota(jnp.int32,(nb,128),0)
    d=jnp.sum(jnp.where(lane==rw,X,0.0),axis=1,keepdims=True)
    return X[:,nb:2*nb]*lax.rsqrt(d)
def orth(a_ref,t_ref,R,inv=inv_diag1):
    n=R//NB
    lane=lax.broadcasted_iota(jnp.int32,(NB,128),1)
    rw=lax.broadcasted_iota(jnp.int32,(NB,128),0)
    for k in range(n):
        rows=slice(k*NB,(k+1)*NB)
        base=k*NB//128*128; off=k*NB-base
        D=a_ref[rows,base:base+128]
        if off: D=pltpu.roll(D,128-off,1)
        X=jnp.where(lane<NB,D,jnp.where(lane-NB==rw,1.0,0.0))
        W=inv(X)
        if k<n-1:
            RA=dot(W,a_ref[rows,:])
            Q=dot(RA[:,:R],RA,TN)
            s=(k+1)*NB
            a_ref[s:,:]=a_ref[s:,:]-Q[s:,:]
        RT=dot(W,t_ref[rows,:])
        t_ref[rows,:]=RT
        if k<n-1:
            Q=dot(RA[:,:R],RT,TN)
            t_ref[s:,:]=t_ref[s:,:]-Q[s:,:]
def subspace(g_ref,a_ref,t_ref,R,iters,inv=inv_diag1):
    for it in range(iters):
        T=dot(t_ref[...],g_ref[...])
        t_ref[...]=T
        a_ref[:,:R]=dot(T,T,NT)
        orth(a_ref,t_ref,R,inv)
PAIRS=[(i,j) for i in range(5) for j in range(i,5)]
def unpack(p_ref,g_ref):
    for q,(i,j) in enumerate(PAIRS):
        b=p_ref[q]
        g_ref[i*128:(i+1)*128,j*128:(j+1)*128]=b
        if i!=j: g_ref[j*128:(j+1)*128,i*128:(i+1)*128]=b.T
def final_kernel(p_ref,s_ref,u_ref,basis_ref,core_ref,g_ref,a_ref,t_ref,*,inv=inv_diag1,corehi=HI):
    R=s_ref.shape[0]
    t_ref[...]=s_ref[...]
    unpack(p_ref,g_ref)
    a_ref[...]=jnp.zeros_like(a_ref)
    subspace(g_ref,a_ref,t_ref,R,2,inv)
    T=t_ref[...]
    basis_ref[...]=T
    for q in range(u_ref.shape[1]//2):
        U=jnp.concatenate([u_ref[:,2*q].reshape(640,128),u_ref[:,2*q+1].reshape(640,128)],axis=1)
        C=dot(T,U,NN,corehi)
        core_ref[2*q]=C[:,:128]; core_ref[2*q+1]=C[:,128:]
def final(p,s,u,**kw):
    return pl.pallas_call(functools.partial(final_kernel,**kw),
        out_shape=(jax.ShapeDtypeStruct((160,640),f32),jax.ShapeDtypeStruct((u.shape[1],160,128),f32)),
        in_specs=[pl.BlockSpec(memory_space=pltpu.VMEM)]*3,
        out_specs=(pl.BlockSpec(memory_space=pltpu.VMEM),)*2,
        scratch_shapes=[pltpu.VMEM((640,640),f32),pltpu.VMEM((160,256),f32),pltpu.VMEM((160,640),f32)],
        compiler_params=pltpu.CompilerParams(vmem_limit_bytes=48<<20))(p,s,u)
def split(x,n):
    out=[]
    for i in range(n):
        h=x.astype(jnp.bfloat16); out.append(h)
        if i<n-1: x=x-h.astype(f32)
    return out
def gram_kernel(u_ref,o_ref,*sc,n):
    np_=u_ref.shape[1]
    for p in range(np_):
        x=u_ref[:,p].reshape(640,128)
        for r,h in zip(sc,split(x,n)): r[:,p*128:(p+1)*128]=h
    prods=[(0,0),(0,1),(1,0)] if n==2 else [(0,0),(0,1),(1,0),(1,1),(0,2),(2,0)]
    q=0
    for i in range(5):
        acc=None
        for a,b in reversed(prods):
            t=lax.dot_general(sc[a][i*128:(i+1)*128,:],sc[b][i*128:,:],NT,preferred_element_type=f32)
            acc=t if acc is None else acc+t
        for j in range(i,5):
            o_ref[q]=acc[:,(j-i)*128:(j-i+1)*128]; q+=1
def gram(u,n=3):
    return pl.pallas_call(functools.partial(gram_kernel,n=n),
        out_shape=jax.ShapeDtypeStruct((15,128,128),f32),
        in_specs=[pl.BlockSpec(memory_space=pltpu.VMEM)],
        out_specs=pl.BlockSpec(memory_space=pltpu.VMEM),
        scratch_shapes=[pltpu.VMEM((640,u.shape[1]*128),jnp.bfloat16)]*n,
        compiler_params=pltpu.CompilerParams(vmem_limit_bytes=48<<20))(u)


FIBRE = ("y", "c")
NEAR = ("c", "x")
FAR = ("y", "z")


def exchange(pieces, axes):
    return lax.all_to_all(pieces, axes, 0, 0, tiled=True)


def sum_everywhere(packed):
    with jax.named_scope("reduce_near"):
        pieces = packed.reshape(8, 240, 128)
        mine = exchange(pieces, NEAR).sum(0)
    with jax.named_scope("reduce_far"):
        mine = jnp.pad(mine, ((0, 16), (0, 0))).reshape(64, 4, 128)
        mine = exchange(mine, FAR).sum(0)
    with jax.named_scope("gather_far"):
        mine = exchange(jnp.broadcast_to(mine, (64, 4, 128)), FAR)
        mine = mine.reshape(256, 128)[:240]
    with jax.named_scope("gather_near"):
        mine = lax.all_gather(mine, "x", axis=0, tiled=True)
        mine = lax.all_gather(mine, "c", axis=0, tiled=True)
    return mine.reshape(15, 128, 128)


def shards(field, start):
    with jax.named_scope("regroup"):
        pieces = field.transpose(1, 0, 2).reshape(16, 10, 40, 128)
        held = exchange(pieces, FIBRE)
    with jax.named_scope("gram"):
        local = gram(held)
    packed = sum_everywhere(local)
    with jax.named_scope("subspace"):
        basis, core = final(packed, start.T, held)
    return basis.T, core.transpose(1, 0, 2)


def solution(mesh):
    inner = jax.sharding.Mesh(mesh.devices.reshape(8, 2, 4, 8), ("y", "c", "x", "z"))
    return jax.shard_map(
        shards,
        mesh=inner,
        in_specs=(P(FIBRE, None, ("x", "z")), P()),
        out_specs=(P(), P(None, FIBRE, ("x", "z"))),
        check_vma=False,
    )
```

time: 508 us -> 216 us (0.43)
  waiting for transfers between devices: 266 us -> 0 us
  other arithmetic: 91.8 us -> 1.34 us
  blocking collectives: 86 us -> 160 us
  Pallas kernels: 0 us -> 48.6 us
  matrix products: 26.1 us -> 0 us
  between operations: 17.1 us -> 0.66 us
  local copies, waits for them, and re-layouts: 17.8 us -> 4.87 us
    psum x1 -> x0, waiting for transfers between devices: 266 us -> none  [shards(): gram = lax.psum(local_gram, ('fibre', 'col'))]
    another operation x25 -> x0, other arithmetic: 91.8 us -> none  [the longest x14 51.6 us: subspace(): factor = jnp.linalg.cholesky(small)]
    all_to_all x1 -> x4, blocking collectives: 86 us -> 142 us  [exchange(): return lax.all_to_all(pieces, axes, 0, 0, tiled=True)]
    pallas_call x0 -> x2, Pallas kernels: none -> 48.6 us  [the longest x1 39.9 us: final(): pl.pallas_call(functools.partial(final_kernel, **kw), out_shape=(jax.Shap...]
    dot_general x6 -> x0, matrix products: 23.4 us -> none  [the longest x1 10.5 us: shards(): jnp.dot(unfolded, unfolded.T, precision=lax.Precision.HIGHEST, preferred_...]
    all_gather x0 -> x2, blocking collectives: none -> 18.1 us  [the longest x1 9.83 us: sum_everywhere(): mine = lax.all_gather(mine, 'x', axis=0, tiled=True)]
    unnamed x10 -> x2, local copies, waits for them, and re-layouts: 12 us -> 1 us
  transfers between devices with their start and end apart: 1 -> 0, of which waited for: 1 -> 0; matrix products, arithmetic and copies ran while one was open for 2% -> 0% of each run, Pallas kernels for 0% -> 0%
where the time goes in v1:
time: 216 us
  blocking collectives  160 us (74%)
  Pallas kernels  48.6 us (22%)
  local copies, waits for them, and re-layouts  4.87 us (2%)
    all_to_all x4, blocking collectives, exchange(): return lax.all_to_all(pieces, axes, 0, 0, tiled=True)  142 us
    pallas_call x1, Pallas kernels, final(): pl.pallas_call(functools.partial(final_kernel, **kw), out_shape=(jax.Shap...  39.9 us
    all_gather x1, blocking collectives, sum_everywhere(): mine = lax.all_gather(mine, 'x', axis=0, tiled=True)  9.83 us
    pallas_call x1, Pallas kernels, gram(): pl.pallas_call(functools.partial(gram_kernel, n=n), out_shape=jax.ShapeDt...  8.71 us
    all_gather x1, blocking collectives, sum_everywhere(): mine = lax.all_gather(mine, 'c', axis=0, tiled=True)  8.25 us

profile of v1, /device:TPU:1, one launch (start us, length us, event | category | flops | bytes accessed | tf_op | source)
XLA Modules:
  0.0 215.7 jit_solution(17719359397840252129)
XLA Ops:
  0.6 3.8 %copy.6 = f32[160,40,128]{2,1,0:T(8,128)S(1)} copy(f32[160,40,128]{2,0,1:T(8,128)} %bitcast.13) | data formatting | bytes 6553600 | tf_op jit(solution)/shard_map/regroup/transpose | solution.py:132
  4.5 85.9 %all_to_all.20.u_ref = f32[16,10,40,128]{3,2,1,0:T(8,128)S(1)} all-to-all(f32[16,10,40,128]{3,2,1,0:T(8,128)S(1)} %bitcast.12), channel_id=1, replica_groups=mesh['y'=8,'c'=2,'x'=4,'z'=8] {'y','c'}, dimensions={0} | all-to-all | bytes 6553600 | tf_op jit(solution)/shard_map/regroup/all_to_all | solution.py:111
  90.3 8.7 %gram.1 = f32[15,128,128]{2,1,0:T(8,128)S(1)} custom-call(f32[16,10,40,128]{3,2,1,0:T(8,128)S(1)} %all_to_all.20.u_ref), custom_call_target="tpu_custom_call" | custom-call | tf_op jit(solution)/shard_map/gram/pallas_call | solution.py:97
  99.1 17.6 %all_to_all.21 = f32[8,240,128]{2,1,0:T(8,128)} all-to-all(f32[8,240,128]{2,1,0:T(8,128)S(1)} %bitcast.10), channel_id=1, replica_groups=mesh['y'=8,'c'=2,'x'=4,'z'=8] {'c','x'}, dimensions={0} | all-to-all | bytes 1966080 | tf_op jit(solution)/shard_map/reduce_near/all_to_all | solution.py:111
  116.6 1.3 reduce_sum.18
  117.9 23.2 %all_to_all.22 = f32[64,4,128]{2,1,0:T(4,128)S(1)} all-to-all(f32[64,4,128]{2,1,0:T(4,128)S(1)} %bitcast.14), channel_id=1, replica_groups=mesh['y'=8,'c'=2,'x'=4,'z'=8] {'y','z'}, dimensions={0} | all-to-all | bytes 262144 | tf_op jit(solution)/shard_map/reduce_far/all_to_all | solution.py:111
  141.1 0.1 reduce_sum.19
  141.2 15.6 %all_to_all.23 = f32[64,4,128]{2,1,0:T(4,128)S(1)} all-to-all(f32[64,4,128]{2,1,0:T(4,128)S(1)} %broadcast_in_dim.3), channel_id=1, replica_groups=mesh['y'=8,'c'=2,'x'=4,'z'=8] {'y','z'}, dimensions={0} | all-to-all | bytes 262144 | tf_op jit(solution)/shard_map/gather_far/all_to_all | solution.py:111
  156.8 9.8 %all_gather.6 = f32[960,128]{1,0:T(8,128)S(1)} all-gather(f32[240,128]{1,0:T(8,128)S(1)} %bitcast.15), channel_id=1, replica_groups=mesh['y'=8,'c'=2,'x'=4,'z'=8] {'x'}, dimensions={0}, use_global_device_ids=true | all-gather | bytes 614400 | tf_op jit(solution)/shard_map/gather_near/all_gather | solution.py:125
  166.6 8.2 %all_gather.7 = f32[1920,128]{1,0:T(8,128)S(1)} all-gather(f32[960,128]{1,0:T(8,128)S(1)} %all_gather.6), channel_id=1, replica_groups=mesh['y'=8,'c'=2,'x'=4,'z'=8] {'c'}, dimensions={0}, use_global_device_ids=true | all-gather | bytes 1474560 | tf_op jit(solution)/shard_map/gather_near/all_gather | solution.py:126
  174.8 0.0 copy-start
  174.8 1.0 copy-done
  175.8 39.9 %subspace.1 = (f32[160,640]{1,0:T(8,128)}, f32[10,160,128]{2,1,0:T(8,128)}) custom-call(f32[15,128,128]{2,1,0:T(8,128)S(1)} %bitcast.9, f32[160,640]{1,0:T(8,128)S(1)} %bitcast.11, f32[16,10,40,128]{3,2,1,0:T(8,128)S(1)} %all_to_all.20.u_ref), custom_call_target="tpu_custom_call" | custom-call | tf_op jit(solution)/shard_map/subspace/pallas_call | solution.py:70
  (3 shorter events, 0.0 us)
Async XLA Ops:
  174.8 1.0 copy-start

commit v2 on v0

v2 whole, which is shorter than its diff:
```python
import functools

import jax
import jax.numpy as jnp
from jax import lax
from jax.experimental import pallas as pl
from jax.experimental.pallas import tpu as pltpu
from jax.sharding import PartitionSpec as P

ITERS = 2
FIBRE = ("y", "c")
FAR = ("x", "y", "z")
SWAP = [(0, 1), (1, 0)]
NB = 40
STEP = 8
PAIRS = [(i, j) for i in range(5) for j in range(i, 5)]
VMEM = pl.BlockSpec(memory_space=pltpu.VMEM)
SMEM = pl.BlockSpec(memory_space=pltpu.SMEM)
ANY = pl.BlockSpec(memory_space=pl.ANY)
WHOLE = pltpu.CompilerParams(vmem_limit_bytes=60 << 20)
BIG = pltpu.CompilerParams(vmem_limit_bytes=24 << 20)
BF = jnp.bfloat16
F32 = jnp.float32
NN = (((1,), (0,)), ((), ()))
NT = (((1,), (1,)), ((), ()))
TN = (((0,), (0,)), ((), ()))


def dot(a, b, dims=NN):
    return lax.dot_general(
        a, b, dims, precision=lax.Precision.HIGHEST, preferred_element_type=F32
    )


def dot16(a, b, dims=NN):
    return lax.dot_general(a, b, dims, preferred_element_type=F32)


def halves(x):
    high = x.astype(BF)
    return high, (x - high.astype(F32)).astype(BF)


def regroup_kernel(field_ref, out_ref, sem):
    for p in range(field_ref.shape[1]):
        pltpu.make_async_copy(field_ref.at[:, p], out_ref.at[p], sem).start()
    pltpu.make_async_copy(out_ref, out_ref, sem).wait()


def regroup(field):
    rows, cells, lanes = field.shape
    return pl.pallas_call(
        regroup_kernel,
        out_shape=jax.ShapeDtypeStruct((cells, rows, lanes), F32),
        in_specs=[ANY],
        out_specs=ANY,
        scratch_shapes=[pltpu.SemaphoreType.DMA],
        compiler_params=WHOLE,
    )(field)


def gram_kernel(core_ref, held_ref, out_ref, high_ref, low_ref):
    for p in range(held_ref.shape[1]):
        x = held_ref[:, p].reshape(640, 128)
        high_ref[:, p * 128 : (p + 1) * 128], low_ref[:, p * 128 : (p + 1) * 128] = halves(x)
    core = core_ref[0]
    for slot in range(2):
        out_ref[slot, 960:, :] = jnp.zeros((64, 128), F32)
    block = 0
    for i in range(5):
        rows = slice(i * 128, (i + 1) * 128)
        both = jnp.concatenate([high_ref[rows, :], low_ref[rows, :]])
        by_high = dot16(both, high_ref[i * 128 :, :], NT)
        by_low = dot16(both, low_ref[i * 128 :, :], NT)
        product = (by_high[128:] + by_low[:128] + by_low[128:]) + by_high[:128]
        for j in range(5 - i):
            for part in range(2):
                piece = 2 * block + part
                at = piece % 15 * 64
                slot = core if piece < 15 else 1 - core
                out_ref[slot, at : at + 64, :] = product[
                    part * 64 : (part + 1) * 64, j * 128 : (j + 1) * 128
                ]
            block += 1


def local_gram(core, held):
    flat = jax.ShapeDtypeStruct((640, held.shape[1] * 128), BF)
    return pl.pallas_call(
        gram_kernel,
        out_shape=(jax.ShapeDtypeStruct((2, 1024, 128), F32), flat, flat),
        in_specs=[SMEM, VMEM],
        out_specs=(VMEM,) * 3,
        compiler_params=BIG,
    )(core, held)


def eliminate(square, w_ref):
    count = NB // 8
    tiles = [square[8 * t : 8 * t + 8] for t in range(count)]
    for j in range(0, NB, STEP):
        t0 = j // 8
        cols = [
            [jnp.broadcast_to(tiles[t][:, j + k : j + k + 1], (8, 128)) for t in range(t0, count)]
            for k in range(STEP)
        ]
        rows = [tiles[(j + k) // 8][(j + k) % 8 : (j + k) % 8 + 1, :] for k in range(STEP)]
        a = {
            (i, k): cols[k][(j + i) // 8 - t0][(j + i) % 8 : (j + i) % 8 + 1, :]
            for k in range(STEP)
            for i in range(k, STEP)
        }
        for k in range(STEP):
            scale = lax.rsqrt(a[k, k])
            rows[k] = rows[k] * scale
            for i in range(k + 1, STEP):
                a[i, k] = a[i, k] * scale
            for i in range(k + 1, STEP):
                for m in range(k + 1, i + 1):
                    a[i, m] = a[i, m] - a[i, k] * a[m, k]
            for i in range(k + 1, STEP):
                rows[i] = rows[i] - a[i, k] * rows[k]
            cols[k] = [c * scale for c in cols[k]]
            for i in range(k + 1, STEP):
                cols[i] = [c - a[i, k] * w for c, w in zip(cols[i], cols[k])]
            w_ref[j + k : j + k + 1, :] = rows[k]
        for t in range((j + STEP) // 8, count):
            change = cols[0][t - t0] * rows[0]
            for k in range(1, STEP):
                change = change + cols[k][t - t0] * rows[k]
            tiles[t] = tiles[t] - change
    return w_ref[:, NB : 2 * NB]


def orthonormalize(a_ref, t_ref, w_ref):
    rank = t_ref.shape[0]
    lane = lax.broadcasted_iota(jnp.int32, (NB, 128), 1)
    row = lax.broadcasted_iota(jnp.int32, (NB, 128), 0)
    for k in range(rank // NB):
        own = slice(k * NB, (k + 1) * NB)
        rest = (k + 1) * NB
        base = k * NB // 128 * 128
        off = k * NB - base
        block = a_ref[own, base : base + 128]
        if off:
            block = pltpu.roll(block, 128 - off, 1)
        if off + NB > 128:
            after = pltpu.roll(a_ref[own, base + 128 : base + 256], 128 - off, 1)
            block = jnp.where(lane < 128 - off, block, after)
        square = jnp.where(lane < NB, block, jnp.where(lane - NB == row, 1.0, 0.0))
        w = eliminate(square, w_ref.at[k % 2])
        if rest < rank:
            upper = dot(w, a_ref[own, :])
            change = dot(upper[:, :rank], upper, TN)
            a_ref[rest:, :] = a_ref[rest:, :] - change[rest:, :]
        solved = dot(w, t_ref[own, :])
        t_ref[own, :] = solved
        if rest < rank:
            change = dot(upper[:, :rank], solved, TN)
            t_ref[rest:, :] = t_ref[rest:, :] - change[rest:, :]


def subspace_kernel(
    packed_ref, start_ref, high_ref, low_ref, basis_ref, core_ref, g_ref, a_ref, t_ref, w_ref
):
    rank = start_ref.shape[0]
    for q, (i, j) in enumerate(PAIRS):
        block = packed_ref[q]
        g_ref[i * 128 : (i + 1) * 128, j * 128 : (j + 1) * 128] = block
        if i != j:
            g_ref[j * 128 : (j + 1) * 128, i * 128 : (i + 1) * 128] = block.T
    t_ref[...] = start_ref[...]
    a_ref[...] = jnp.zeros_like(a_ref)
    for _ in range(ITERS):
        image = dot(t_ref[...], g_ref[...])
        t_ref[...] = image
        a_ref[:, :rank] = dot(image, image, NT)
        orthonormalize(a_ref, t_ref, w_ref)
    basis = t_ref[...]
    basis_ref[...] = basis
    high, low = halves(basis)
    both = jnp.concatenate([high, low])
    for q in range(high_ref.shape[1] // 256):
        lanes = slice(q * 256, (q + 1) * 256)
        by_high = dot16(both, high_ref[:, lanes])
        by_low = dot16(high, low_ref[:, lanes])
        product = (by_high[rank:] + by_low) + by_high[:rank]
        core_ref[2 * q] = product[:, :128]
        core_ref[2 * q + 1] = product[:, 128:]


def subspace_and_core(packed, start, high, low):
    rank, rows = start.shape
    cells = high.shape[1] // 128
    return pl.pallas_call(
        subspace_kernel,
        out_shape=(
            jax.ShapeDtypeStruct((rank, rows), F32),
            jax.ShapeDtypeStruct((cells, rank, 128), F32),
        ),
        in_specs=[VMEM] * 4,
        out_specs=(VMEM,) * 2,
        scratch_shapes=[
            pltpu.VMEM((rows, rows), F32),
            pltpu.VMEM((rank, 256), F32),
            pltpu.VMEM((rank, rows), F32),
            pltpu.VMEM((2, NB, 128), F32),
        ],
        compiler_params=BIG,
    )(packed, start, high, low)


def exchange(pieces, axes):
    return lax.all_to_all(pieces, axes, 0, 0, tiled=True)


def shards(field, start):
    with jax.named_scope("regroup"):
        pieces = regroup(field).reshape(16, 10, 40, 128)
        held = exchange(pieces, FIBRE)
    with jax.named_scope("gram"):
        core = lax.axis_index("c").astype(jnp.int32).reshape(1)
        parts, high, low = local_gram(core, held)
    with jax.named_scope("reduce_pair"):
        mine = parts[0] + lax.ppermute(parts[1], "c", SWAP)
    with jax.named_scope("reduce_far"):
        mine = exchange(mine.reshape(256, 4, 128), FAR).sum(0)
    with jax.named_scope("gather_far"):
        mine = exchange(jnp.broadcast_to(mine, (256, 4, 128)), FAR)
        mine = mine[:240].reshape(960, 128)
    with jax.named_scope("gather_pair"):
        packed = lax.all_gather(mine, "c", axis=0, tiled=True).reshape(15, 128, 128)
    with jax.named_scope("subspace"):
        basis, core = subspace_and_core(packed, start.T, high, low)
    return basis.T, core.transpose(1, 0, 2)


def solution(mesh):
    inner = jax.sharding.Mesh(mesh.devices.reshape(8, 2, 4, 8), ("y", "c", "x", "z"))
    return jax.shard_map(
        shards,
        mesh=inner,
        in_specs=(P(FIBRE, None, ("x", "z")), P()),
        out_specs=(P(), P(None, FIBRE, ("x", "z"))),
        check_vma=False,
    )
```

time: 508 us -> 286 us (0.56)
  waiting for transfers between devices: 266 us -> 75.4 us
  Pallas kernels: 0 us -> 122 us
  other arithmetic: 91.8 us -> 1.4 us
  matrix products: 26.1 us -> 0 us
  between operations: 17.1 us -> 0.7 us
  blocking collectives: 86 us -> 70.3 us
  local copies, waits for them, and re-layouts: 17.8 us -> 2.47 us
  starting transfers between devices: 0.04 us -> 13.5 us
    psum x1 -> x0, waiting for transfers between devices: 266 us -> none  [shards(): gram = lax.psum(local_gram, ('fibre', 'col'))]
    pallas_call x0 -> x3, Pallas kernels: none -> 122 us  [the longest x1 100 us: regroup(): pl.pallas_call(regroup_kernel, out_shape=jax.ShapeDtypeStruct((cells, row...]
    another operation x25 -> x0, other arithmetic: 91.8 us -> none  [the longest x14 51.6 us: subspace(): factor = jnp.linalg.cholesky(small)]
    all_to_all x0 -> x1, waiting for transfers between devices: none -> 73.9 us  [exchange(): return lax.all_to_all(pieces, axes, 0, 0, tiled=True)]
    dot_general x6 -> x0, matrix products: 23.4 us -> none  [the longest x1 10.5 us: shards(): jnp.dot(unfolded, unfolded.T, precision=lax.Precision.HIGHEST, preferred_...]
    all_to_all x1 -> x2, blocking collectives: 86 us -> 64.5 us  [exchange(): return lax.all_to_all(pieces, axes, 0, 0, tiled=True)]
    all_to_all x0 -> x1, starting transfers between devices: none -> 10.4 us  [exchange(): return lax.all_to_all(pieces, axes, 0, 0, tiled=True)]
    unnamed x10, local copies, waits for them, and re-layouts: 12 us -> 2.33 us
  transfers between devices with their start and end apart: 1 -> 2, of which waited for: 1 -> 2; matrix products, arithmetic and copies ran while one was open for 2% -> 0% of each run, Pallas kernels for 0% -> 0%
where the time goes in v2:
time: 286 us; the launch traced here: 285 us
  Pallas kernels  122 us (43%)
  waiting for transfers between devices  75.4 us (26%)
  blocking collectives  70.3 us (25%)
  starting transfers between devices  13.5 us (5%)
    pallas_call x1, Pallas kernels, regroup(): pl.pallas_call(regroup_kernel, out_shape=jax.ShapeDtypeStruct((cells, row...  100 us
    all_to_all x1, waiting for transfers between devices, exchange(): return lax.all_to_all(pieces, axes, 0, 0, tiled=True)  73.9 us
    all_to_all x2, blocking collectives, exchange(): return lax.all_to_all(pieces, axes, 0, 0, tiled=True)  64.5 us
    pallas_call x1, Pallas kernels, subspace_and_core(): pl.pallas_call(subspace_kernel, out_shape=(jax.ShapeDtypeStruct((rank, ro...  18 us
    all_to_all x1, starting transfers between devices, exchange(): return lax.all_to_all(pieces, axes, 0, 0, tiled=True)  10.4 us
    all_gather x1, blocking collectives, shards(): packed = lax.all_gather(mine, 'c', axis=0, tiled=True).reshape(15, 128, 128)  5.86 us
  transfers between devices with their start and end apart: 2, of which 2 were waited for; matrix products, arithmetic and copies ran while one was open for 0% of the time, Pallas kernels for 0%

profile of v2, /device:TPU:1, one launch (start us, length us, event | category | flops | bytes accessed | tf_op | source)
XLA Modules:
  0.0 285.4 jit_solution(3377900093521559925)
XLA Ops:
  0.6 100.4 %regroup.1 = f32[160,40,128]{2,1,0:T(8,128)} custom-call(f32[40,160,128]{2,1,0:T(8,128)} %field_ref.1), custom_call_target="tpu_custom_call" | custom-call | tf_op jit(solution)/shard_map/regroup/pallas_call | solution.py:52
  101.0 10.4 %all-to-all-start = ((f32[16,10,40,128]{3,2,1,0:T(8,128)}), f32[16,10,40,128]{3,2,1,0:T(8,128)S(1)}, u32[]{:S(2)}, u32[]{:S(2)}) async-start(f32[16,10,40,128]{3,2,1,0:T(8,128)} %bitcast.14), calls=%async_computation | async-start | bytes 6553600 | tf_op jit(solution)/shard_map/regroup/all_to_all | solution.py:214
  111.5 73.9 %all-to-all-done.held_ref = f32[16,10,40,128]{3,2,1,0:T(8,128)S(1)} async-done(((f32[16,10,40,128]{3,2,1,0:T(8,128)}), f32[16,10,40,128]{3,2,1,0:T(8,128)S(1)}, u32[]{:S(2)}, u32[]{:S(2)}) %all-to-all-start) | async-done | bytes 3276832 | tf_op jit(solution)/shard_map/regroup/all_to_all | solution.py:214
  185.4 3.3 %gram.1 = (f32[2,1024,128]{2,1,0:T(8,128)S(1)}, bf16[640,1280]{1,0:T(8,128)(2,1)S(1)}, bf16[640,1280]{1,0:T(8,128)(2,1)S(1)}) custom-call(s32[1]{0:T(128)} %bitcast.core_ref, f32[16,10,40,128]{3,2,1,0:T(8,128)S(1)} %all-to-all-done.held_ref), custom_call_target="tpu_custom_call" | custom-call | tf_op jit(solution)/shard_map/gram/pallas_call | solution.py:89
  188.6 0.0 copy-start
  188.6 1.2 copy-done
  189.8 0.0 copy-start.2
  189.8 1.2 copy-done.2
  191.0 0.0 copy-start.1
  191.0 0.0 copy-start.3
  191.0 3.0 %collective-permute-start = (f32[1024,128]{1,0:T(8,128)S(1)}, f32[1024,128]{1,0:T(8,128)S(1)}, u32[]{:S(2)}, u32[]{:S(2)}) collective-permute-start(f32[1024,128]{1,0:T(8,128)S(1)} %slice_bitcast_fusion), channel_id=1, source_target_pairs={{0,32},{32,0},{1,33},{33,1},{2,34},{34,2},{3,35},{35,3},{4,36},{36... | collective-permute-start | bytes 1572872 | tf_op jit(solution)/shard_map/reduce_pair/ppermute | solution.py:225
  194.1 1.5 collective-permute-done
  195.6 0.1 bitcast_add_fusion
  195.7 36.3 %all_to_all.15 = f32[256,4,128]{2,1,0:T(4,128)} all-to-all(f32[256,4,128]{2,1,0:T(4,128)S(1)} %bitcast.15), channel_id=1, replica_groups=mesh['y'=8,'c'=2,'x'=4,'z'=8] {'x','y','z'}, dimensions={0} | all-to-all | bytes 1048576 | tf_op jit(solution)/shard_map/reduce_far/all_to_all | solution.py:214
  232.0 1.3 reduce_sum.9
  233.3 0.0 copy-start.4
  233.3 0.1 broadcast_in_dim.3
  233.4 28.2 %all_to_all.16 = f32[256,4,128]{2,1,0:T(4,128)S(1)} all-to-all(f32[256,4,128]{2,1,0:T(4,128)S(1)} %broadcast_in_dim.3), channel_id=1, replica_groups=mesh['y'=8,'c'=2,'x'=4,'z'=8] {'x','y','z'}, dimensions={0} | all-to-all | bytes 1048576 | tf_op jit(solution)/shard_map/gather_far/all_to_all | solution.py:214
  261.6 5.9 %all_gather.3 = f32[1920,128]{1,0:T(8,128)S(1)} all-gather(f32[960,128]{1,0:T(8,128)S(1)} %bitcast.16), channel_id=1, replica_groups=mesh['y'=8,'c'=2,'x'=4,'z'=8] {'c'}, dimensions={0}, use_global_device_ids=true | all-gather | bytes 1474560 | tf_op jit(solution)/shard_map/gather_pair/all_gather | solution.py:232
  267.5 0.0 copy-done.1
  267.5 0.0 copy-done.3
  267.5 0.0 copy-done.4
  267.5 18.0 %subspace.1 = (f32[160,640]{1,0:T(8,128)}, f32[10,160,128]{2,1,0:T(8,128)}) custom-call(f32[15,128,128]{2,1,0:T(8,128)S(1)} %bitcast.12, f32[160,640]{1,0:T(8,128)S(1)} %bitcast.13, bf16[640,1280]{1,0:T(8,128)(2,1)S(1)} %copy-done.1, bf16[640,1280]{1,0:T(8,128)(2,1)S(1)} %copy-done.3), custom_call_target="tpu_custom_call" | custom-call | tf_op jit(solution)/shard_map/subspace/pallas_call | solution.py:195
  (2 shorter events, 0.1 us)
Async XLA Ops:
  101.0 84.3 %all-to-all-start = ((f32[16,10,40,128]{3,2,1,0:T(8,128)}), f32[16,10,40,128]{3,2,1,0:T(8,128)S(1)}, u32[]{:S(2)}, u32[]{:S(2)}) async-start(f32[16,10,40,128]{3,2,1,0:T(8,128)} %bitcast.14), calls=%async_computation | async-start | bytes 6553600 | tf_op jit(solution)/shard_map/regroup/all_to_all | solution.py:214
  188.6 1.2 copy-start
  189.8 1.2 copy-start.2
  191.0 76.5 %copy-start.1 = (bf16[640,1280]{1,0:T(8,128)(2,1)S(1)}, bf16[640,1280]{1,0:T(8,128)(2,1)}, u32[]{:S(2)}) copy-start(bf16[640,1280]{1,0:T(8,128)(2,1)} %copy-done) | copy-start | bytes 4915204
  191.0 76.4 %copy-start.3 = (bf16[640,1280]{1,0:T(8,128)(2,1)S(1)}, bf16[640,1280]{1,0:T(8,128)(2,1)}, u32[]{:S(2)}) copy-start(bf16[640,1280]{1,0:T(8,128)(2,1)} %copy-done.2) | copy-start | bytes 4915204
  191.0 4.6 %collective-permute-start = (f32[1024,128]{1,0:T(8,128)S(1)}, f32[1024,128]{1,0:T(8,128)S(1)}, u32[]{:S(2)}, u32[]{:S(2)}) collective-permute-start(f32[1024,128]{1,0:T(8,128)S(1)} %slice_bitcast_fusion), channel_id=1, source_target_pairs={{0,32},{32,0},{1,33},{33,1},{2,34},{34,2},{3,35},{35,3},{4,36},{36... | collective-permute-start | bytes 1572872 | tf_op jit(solution)/shard_map/reduce_pair/ppermute | solution.py:225
  233.3 34.2 %copy-start.4 = (f32[640,160]{0,1:T(8,128)S(1)}, f32[640,160]{0,1:T(8,128)}, u32[]{:S(2)}) copy-start(f32[640,160]{0,1:T(8,128)} %param.3) | copy-start | bytes 1228804

commit v3 on v2

--- a/solution.py
+++ b/solution.py
@@ -9,15 +9,15 @@
 
 ITERS = 2
 FIBRE = ("y", "c")
-FAR = ("x", "y", "z")
+PLANE = ("z", "x")
 SWAP = [(0, 1), (1, 0)]
 NB = 40
 STEP = 8
 PAIRS = [(i, j) for i in range(5) for j in range(i, 5)]
 VMEM = pl.BlockSpec(memory_space=pltpu.VMEM)
+HBM = pl.BlockSpec(memory_space=pltpu.HBM)
 SMEM = pl.BlockSpec(memory_space=pltpu.SMEM)
-ANY = pl.BlockSpec(memory_space=pl.ANY)
-WHOLE = pltpu.CompilerParams(vmem_limit_bytes=60 << 20)
+WHOLE = pltpu.CompilerParams(vmem_limit_bytes=56 << 20)
 BIG = pltpu.CompilerParams(vmem_limit_bytes=24 << 20)
 BF = jnp.bfloat16
 F32 = jnp.float32
@@ -41,28 +41,32 @@
     return high, (x - high.astype(F32)).astype(BF)
 
 
-def regroup_kernel(field_ref, out_ref, sem):
-    for p in range(field_ref.shape[1]):
-        pltpu.make_async_copy(field_ref.at[:, p], out_ref.at[p], sem).start()
-    pltpu.make_async_copy(out_ref, out_ref, sem).wait()
+def regroup_kernel(field_ref, out_ref):
+    out_ref[...] = jnp.swapaxes(field_ref[...], 0, 1)
 
 
 def regroup(field):
     rows, cells, lanes = field.shape
     return pl.pallas_call(
         regroup_kernel,
+        grid=(rows // 8,),
         out_shape=jax.ShapeDtypeStruct((cells, rows, lanes), F32),
-        in_specs=[ANY],
-        out_specs=ANY,
-        scratch_shapes=[pltpu.SemaphoreType.DMA],
+        in_specs=[pl.BlockSpec((8, cells, lanes), lambda i: (i, 0, 0))],
+        out_specs=pl.BlockSpec((cells, 8, lanes), lambda i: (0, i, 0)),
         compiler_params=WHOLE,
     )(field)
 
 
-def gram_kernel(core_ref, held_ref, out_ref, high_ref, low_ref):
+def gram_kernel(core_ref, held_ref, out_ref, high_out, low_out, high_ref, low_ref, sem):
     for p in range(held_ref.shape[1]):
         x = held_ref[:, p].reshape(640, 128)
         high_ref[:, p * 128 : (p + 1) * 128], low_ref[:, p * 128 : (p + 1) * 128] = halves(x)
+    copies = [
+        pltpu.make_async_copy(high_ref, high_out, sem.at[0]),
+        pltpu.make_async_copy(low_ref, low_out, sem.at[1]),
+    ]
+    for copy in copies:
+        copy.start()
     core = core_ref[0]
     for slot in range(2):
         out_ref[slot, 960:, :] = jnp.zeros((64, 128), F32)
@@ -82,15 +86,22 @@
                     part * 64 : (part + 1) * 64, j * 128 : (j + 1) * 128
                 ]
             block += 1
+    for copy in copies:
+        copy.wait()
 
 
 def local_gram(core, held):
     flat = jax.ShapeDtypeStruct((640, held.shape[1] * 128), BF)
     return pl.pallas_call(
         gram_kernel,
-        out_shape=(jax.ShapeDtypeStruct((2, 1024, 128), F32), flat, flat),
+        out_shape=(jax.ShapeDtypeStruct((2, 1024, 128), F32), pltpu.HBM(flat.shape, BF), pltpu.HBM(flat.shape, BF)),
         in_specs=[SMEM, VMEM],
-        out_specs=(VMEM,) * 3,
+        out_specs=(VMEM, HBM, HBM),
+        scratch_shapes=[
+            pltpu.VMEM(flat.shape, BF),
+            pltpu.VMEM(flat.shape, BF),
+            pltpu.SemaphoreType.DMA((2,)),
+        ],
         compiler_params=BIG,
     )(core, held)
 
@@ -161,9 +172,29 @@
 
 
 def subspace_kernel(
-    packed_ref, start_ref, high_ref, low_ref, basis_ref, core_ref, g_ref, a_ref, t_ref, w_ref
+    packed_ref,
+    start_ref,
+    high_in,
+    low_in,
+    basis_out,
+    core_out,
+    g_ref,
+    a_ref,
+    t_ref,
+    w_ref,
+    high_ref,
+    low_ref,
+    core_ref,
+    sem,
 ):
     rank = start_ref.shape[0]
+    pairs = high_ref.shape[1] // 256
+    loads = [
+        pltpu.make_async_copy(high_in, high_ref, sem.at[0]),
+        pltpu.make_async_copy(low_in, low_ref, sem.at[1]),
+    ]
+    for copy in loads:
+        copy.start()
     for q, (i, j) in enumerate(PAIRS):
         block = packed_ref[q]
         g_ref[i * 128 : (i + 1) * 128, j * 128 : (j + 1) * 128] = block
@@ -177,16 +208,24 @@
         a_ref[:, :rank] = dot(image, image, NT)
         orthonormalize(a_ref, t_ref, w_ref)
     basis = t_ref[...]
-    basis_ref[...] = basis
+    stores = [pltpu.make_async_copy(t_ref, basis_out, sem.at[2])]
+    stores[0].start()
+    for copy in loads:
+        copy.wait()
     high, low = halves(basis)
     both = jnp.concatenate([high, low])
-    for q in range(high_ref.shape[1] // 256):
+    for q in range(pairs):
         lanes = slice(q * 256, (q + 1) * 256)
         by_high = dot16(both, high_ref[:, lanes])
         by_low = dot16(high, low_ref[:, lanes])
         product = (by_high[rank:] + by_low) + by_high[:rank]
         core_ref[2 * q] = product[:, :128]
         core_ref[2 * q + 1] = product[:, 128:]
+        two = pl.ds(2 * q, 2)
+        stores.append(pltpu.make_async_copy(core_ref.at[two], core_out.at[two], sem.at[3 + q]))
+        stores[-1].start()
+    for copy in stores:
+        copy.wait()
 
 
 def subspace_and_core(packed, start, high, low):
@@ -198,16 +237,20 @@
             jax.ShapeDtypeStruct((rank, rows), F32),
             jax.ShapeDtypeStruct((cells, rank, 128), F32),
         ),
-        in_specs=[VMEM] * 4,
-        out_specs=(VMEM,) * 2,
+        in_specs=[VMEM, VMEM, HBM, HBM],
+        out_specs=(HBM, HBM),
         scratch_shapes=[
             pltpu.VMEM((rows, rows), F32),
             pltpu.VMEM((rank, 256), F32),
             pltpu.VMEM((rank, rows), F32),
             pltpu.VMEM((2, NB, 128), F32),
+            pltpu.VMEM(high.shape, BF),
+            pltpu.VMEM(low.shape, BF),
+            pltpu.VMEM((cells, rank, 128), F32),
+            pltpu.SemaphoreType.DMA((3 + cells // 2,)),
         ],
         compiler_params=BIG,
-    )(packed, start, high, low)
+    )(packed, start, *(pltpu.with_memory_space_constraint(v, pltpu.HBM) for v in (high, low)))
 
 
 def exchange(pieces, axes):
@@ -223,11 +266,13 @@
         parts, high, low = local_gram(core, held)
     with jax.named_scope("reduce_pair"):
         mine = parts[0] + lax.ppermute(parts[1], "c", SWAP)
-    with jax.named_scope("reduce_far"):
-        mine = exchange(mine.reshape(256, 4, 128), FAR).sum(0)
-    with jax.named_scope("gather_far"):
-        mine = exchange(jnp.broadcast_to(mine, (256, 4, 128)), FAR)
-        mine = mine[:240].reshape(960, 128)
+    with jax.named_scope("reduce_plane"):
+        mine = exchange(mine.reshape(32, 32, 128), PLANE).sum(0)
+    with jax.named_scope("sum_line"):
+        mine = exchange(jnp.broadcast_to(mine, (8, 32, 128)), "y").sum(0)
+    with jax.named_scope("gather_plane"):
+        mine = exchange(jnp.broadcast_to(mine, (32, 32, 128)), PLANE)
+        mine = mine.reshape(1024, 128)[:960]
     with jax.named_scope("gather_pair"):
         packed = lax.all_gather(mine, "c", axis=0, tiled=True).reshape(15, 128, 128)
     with jax.named_scope("subspace"):

time: 286 us -> 183 us (0.64)
  Pallas kernels: 122 us -> 27.7 us
  blocking collectives: 70.3 us -> 65.6 us
    pallas_call x1, Pallas kernels: 100 us -> 5.46 us  [regroup(): pl.pallas_call(regroup_kernel, grid=(rows // 8,), out_shape=jax.ShapeDtyp...]
    all_to_all x2 -> x3, blocking collectives: 64.5 us -> 57.7 us  [exchange(): return lax.all_to_all(pieces, axes, 0, 0, tiled=True)]
where the time goes in v3:
time: 183 us
  waiting for transfers between devices  75.4 us (41%)
  blocking collectives  65.6 us (36%)
  Pallas kernels  27.7 us (15%)
  starting transfers between devices  13.2 us (7%)
    all_to_all x1, waiting for transfers between devices, exchange(): return lax.all_to_all(pieces, axes, 0, 0, tiled=True)  73.9 us
    all_to_all x3, blocking collectives, exchange(): return lax.all_to_all(pieces, axes, 0, 0, tiled=True)  57.7 us
    pallas_call x1, Pallas kernels, subspace_and_core(): pl.pallas_call(subspace_kernel, out_shape=(jax.ShapeDtypeStruct((rank, ro...  18 us
    all_to_all x1, starting transfers between devices, exchange(): return lax.all_to_all(pieces, axes, 0, 0, tiled=True)  10.4 us
    all_gather x1, blocking collectives, shards(): packed = lax.all_gather(mine, 'c', axis=0, tiled=True).reshape(15, 128, 128)  7.84 us
    pallas_call x1, Pallas kernels, regroup(): pl.pallas_call(regroup_kernel, grid=(rows // 8,), out_shape=jax.ShapeDtyp...  5.46 us
    pallas_call x1, Pallas kernels, local_gram(): pl.pallas_call(gram_kernel, out_shape=(jax.ShapeDtypeStruct((2, 1024, 128...  4.27 us
  transfers between devices with their start and end apart: 2, of which 2 were waited for; matrix products, arithmetic and copies ran while one was open for 0% of the time, Pallas kernels for 0%

profile of v3, /device:TPU:1, one launch (start us, length us, event | category | flops | bytes accessed | tf_op | source)
XLA Modules:
  0.0 183.1 jit_solution(4780771551461031436)
XLA Ops:
  0.6 5.5 %regroup.1 = f32[160,40,128]{2,1,0:T(8,128)} custom-call(f32[40,160,128]{2,1,0:T(8,128)} %field_ref.1), custom_call_target="tpu_custom_call" | custom-call | tf_op jit(solution)/shard_map/regroup/pallas_call | solution.py:50
  6.1 10.4 %all-to-all-start = ((f32[16,10,40,128]{3,2,1,0:T(8,128)}), f32[16,10,40,128]{3,2,1,0:T(8,128)S(1)}, u32[]{:S(2)}, u32[]{:S(2)}) async-start(f32[16,10,40,128]{3,2,1,0:T(8,128)} %bitcast.14), calls=%async_computation | async-start | bytes 6553600 | tf_op jit(solution)/shard_map/regroup/all_to_all | solution.py:257
  16.5 73.9 %all-to-all-done.held_ref = f32[16,10,40,128]{3,2,1,0:T(8,128)S(1)} async-done(((f32[16,10,40,128]{3,2,1,0:T(8,128)}), f32[16,10,40,128]{3,2,1,0:T(8,128)S(1)}, u32[]{:S(2)}, u32[]{:S(2)}) %all-to-all-start) | async-done | bytes 3276832 | tf_op jit(solution)/shard_map/regroup/all_to_all | solution.py:257
  90.4 4.3 %gram.1 = (f32[2,1024,128]{2,1,0:T(8,128)S(1)}, bf16[640,1280]{1,0:T(8,128)(2,1)}, bf16[640,1280]{1,0:T(8,128)(2,1)}) custom-call(s32[1]{0:T(128)} %bitcast.core_ref, f32[16,10,40,128]{3,2,1,0:T(8,128)S(1)} %all-to-all-done.held_ref), custom_call_target="tpu_custom_call" | custom-call | tf_op jit(solution)/shard_map/gram/pallas_call | solution.py:95
  94.7 2.8 %collective-permute-start = (f32[1024,128]{1,0:T(8,128)S(1)}, f32[1024,128]{1,0:T(8,128)S(1)}, u32[]{:S(2)}, u32[]{:S(2)}) collective-permute-start(f32[1024,128]{1,0:T(8,128)S(1)} %slice_bitcast_fusion), channel_id=1, source_target_pairs={{0,32},{32,0},{1,33},{33,1},{2,34},{34,2},{3,35},{35,3},{4,36},{36... | collective-permute-start | bytes 1572872 | tf_op jit(solution)/shard_map/reduce_pair/ppermute | solution.py:268
  97.5 1.5 collective-permute-done
  99.0 0.1 bitcast_add_fusion
  99.1 0.0 copy-start
  99.1 27.5 %all_to_all.20 = f32[32,32,128]{2,1,0:T(8,128)S(1)} all-to-all(f32[32,32,128]{2,1,0:T(8,128)S(1)} %bitcast.15), channel_id=1, replica_groups=mesh['y'=8,'c'=2,'x'=4,'z'=8] {'z','x'}, dimensions={0} | all-to-all | bytes 1048576 | tf_op jit(solution)/shard_map/reduce_plane/all_to_all | solution.py:257
  126.7 12.1 %all_to_all.21 = f32[8,32,128]{2,1,0:T(8,128)S(1)} all-to-all(f32[8,32,128]{2,1,0:T(8,128)S(1)} %broadcast_in_dim.6), channel_id=1, replica_groups=mesh['y'=8,'c'=2,'x'=4,'z'=8] {'y'}, dimensions={0} | all-to-all | bytes 262144 | tf_op jit(solution)/shard_map/sum_line/all_to_all | solution.py:257
  138.8 0.1 broadcast_in_dim.7
  138.9 18.1 %all_to_all.22 = f32[32,32,128]{2,1,0:T(8,128)S(1)} all-to-all(f32[32,32,128]{2,1,0:T(8,128)S(1)} %broadcast_in_dim.7), channel_id=1, replica_groups=mesh['y'=8,'c'=2,'x'=4,'z'=8] {'z','x'}, dimensions={0} | all-to-all | bytes 1048576 | tf_op jit(solution)/shard_map/gather_plane/all_to_all | solution.py:257
  157.0 7.8 %all_gather.3 = f32[1920,128]{1,0:T(8,128)S(1)} all-gather(f32[960,128]{1,0:T(8,128)S(1)} %bitcast.16), channel_id=1, replica_groups=mesh['y'=8,'c'=2,'x'=4,'z'=8] {'c'}, dimensions={0}, use_global_device_ids=true | all-gather | bytes 1474560 | tf_op jit(solution)/shard_map/gather_pair/all_gather | solution.py:277
  164.9 0.0 copy-done
  164.9 18.0 %subspace.1 = (f32[160,640]{1,0:T(8,128)}, f32[10,160,128]{2,1,0:T(8,128)}) custom-call(f32[15,128,128]{2,1,0:T(8,128)S(1)} %bitcast.12, f32[160,640]{1,0:T(8,128)S(1)} %bitcast.13, bf16[640,1280]{1,0:T(8,128)(2,1)} %get-tuple-element.8.high_in, bf16[640,1280]{1,0:T(8,128)(2,1)} %get-tuple-element.9.low_in), custom_call_target="tpu_custom_call" | custom-call | tf_op jit(solution)/shard_map/subspace/pallas_call | solution.py:234
  (5 shorter events, 0.1 us)
Async XLA Ops:
  6.1 84.3 %all-to-all-start = ((f32[16,10,40,128]{3,2,1,0:T(8,128)}), f32[16,10,40,128]{3,2,1,0:T(8,128)S(1)}, u32[]{:S(2)}, u32[]{:S(2)}) async-start(f32[16,10,40,128]{3,2,1,0:T(8,128)} %bitcast.14), calls=%async_computation | async-start | bytes 6553600 | tf_op jit(solution)/shard_map/regroup/all_to_all | solution.py:257
  94.7 4.3 %collective-permute-start = (f32[1024,128]{1,0:T(8,128)S(1)}, f32[1024,128]{1,0:T(8,128)S(1)}, u32[]{:S(2)}, u32[]{:S(2)}) collective-permute-start(f32[1024,128]{1,0:T(8,128)S(1)} %slice_bitcast_fusion), channel_id=1, source_target_pairs={{0,32},{32,0},{1,33},{33,1},{2,34},{34,2},{3,35},{35,3},{4,36},{36... | collective-permute-start | bytes 1572872 | tf_op jit(solution)/shard_map/reduce_pair/ppermute | solution.py:268
  99.1 65.8 %copy-start = (f32[640,160]{0,1:T(8,128)S(1)}, f32[640,160]{0,1:T(8,128)}, u32[]{:S(2)}) copy-start(f32[640,160]{0,1:T(8,128)} %param.3) | copy-start | bytes 1228804

commit v4 on v3

--- a/solution.py
+++ b/solution.py
@@ -13,11 +13,14 @@
 SWAP = [(0, 1), (1, 0)]
 NB = 40
 STEP = 8
-PAIRS = [(i, j) for i in range(5) for j in range(i, 5)]
+UPPER = [20, 21, 22, 23, 24]
+ACROSS = {
+    pair: 2 * at
+    for at, pair in enumerate((i, j) for i in range(5) for j in range(i + 1, 5))
+}
 VMEM = pl.BlockSpec(memory_space=pltpu.VMEM)
 HBM = pl.BlockSpec(memory_space=pltpu.HBM)
 SMEM = pl.BlockSpec(memory_space=pltpu.SMEM)
-WHOLE = pltpu.CompilerParams(vmem_limit_bytes=56 << 20)
 BIG = pltpu.CompilerParams(vmem_limit_bytes=24 << 20)
 BF = jnp.bfloat16
 F32 = jnp.float32
@@ -39,22 +42,6 @@
 def halves(x):
     high = x.astype(BF)
     return high, (x - high.astype(F32)).astype(BF)
-
-
-def regroup_kernel(field_ref, out_ref):
-    out_ref[...] = jnp.swapaxes(field_ref[...], 0, 1)
-
-
-def regroup(field):
-    rows, cells, lanes = field.shape
-    return pl.pallas_call(
-        regroup_kernel,
-        grid=(rows // 8,),
-        out_shape=jax.ShapeDtypeStruct((cells, rows, lanes), F32),
-        in_specs=[pl.BlockSpec((8, cells, lanes), lambda i: (i, 0, 0))],
-        out_specs=pl.BlockSpec((cells, 8, lanes), lambda i: (0, i, 0)),
-        compiler_params=WHOLE,
-    )(field)
 
 
 def gram_kernel(core_ref, held_ref, out_ref, high_out, low_out, high_ref, low_ref, sem):
@@ -68,24 +55,30 @@
     for copy in copies:
         copy.start()
     core = core_ref[0]
-    for slot in range(2):
-        out_ref[slot, 960:, :] = jnp.zeros((64, 128), F32)
-    block = 0
+
+    def put(strip, value):
+        at = strip % 14 * 64
+        out_ref[core if strip < 14 else 1 - core, at : at + 64, :] = value
+
+    lower = []
     for i in range(5):
         rows = slice(i * 128, (i + 1) * 128)
         both = jnp.concatenate([high_ref[rows, :], low_ref[rows, :]])
         by_high = dot16(both, high_ref[i * 128 :, :], NT)
         by_low = dot16(both, low_ref[i * 128 :, :], NT)
         product = (by_high[128:] + by_low[:128] + by_low[128:]) + by_high[:128]
-        for j in range(5 - i):
-            for part in range(2):
-                piece = 2 * block + part
-                at = piece % 15 * 64
-                slot = core if piece < 15 else 1 - core
-                out_ref[slot, at : at + 64, :] = product[
-                    part * 64 : (part + 1) * 64, j * 128 : (j + 1) * 128
-                ]
-            block += 1
+        for j in range(i, 5):
+            block = product[:, (j - i) * 128 : (j - i + 1) * 128]
+            if i == j:
+                put(UPPER[i], block[:64])
+                lower.append(block[64:])
+            else:
+                put(ACROSS[i, j], block[:64])
+                put(ACROSS[i, j] + 1, block[64:])
+    left = lax.broadcasted_iota(jnp.int32, (64, 128), 1) < 64
+    put(25, jnp.where(left, pltpu.roll(lower[1], 64, 1), lower[0]))
+    put(26, jnp.where(left, pltpu.roll(lower[3], 64, 1), lower[2]))
+    put(27, lower[4])
     for copy in copies:
         copy.wait()
 
@@ -94,7 +87,7 @@
     flat = jax.ShapeDtypeStruct((640, held.shape[1] * 128), BF)
     return pl.pallas_call(
         gram_kernel,
-        out_shape=(jax.ShapeDtypeStruct((2, 1024, 128), F32), pltpu.HBM(flat.shape, BF), pltpu.HBM(flat.shape, BF)),
+        out_shape=(jax.ShapeDtypeStruct((2, 896, 128), F32), pltpu.HBM(flat.shape, BF), pltpu.HBM(flat.shape, BF)),
         in_specs=[SMEM, VMEM],
         out_specs=(VMEM, HBM, HBM),
         scratch_shapes=[
@@ -195,11 +188,19 @@
     ]
     for copy in loads:
         copy.start()
-    for q, (i, j) in enumerate(PAIRS):
-        block = packed_ref[q]
+    for (i, j), at in ACROSS.items():
+        block = packed_ref[at * 64 : at * 64 + 128, :]
         g_ref[i * 128 : (i + 1) * 128, j * 128 : (j + 1) * 128] = block
-        if i != j:
-            g_ref[j * 128 : (j + 1) * 128, i * 128 : (i + 1) * 128] = block.T
+        g_ref[j * 128 : (j + 1) * 128, i * 128 : (i + 1) * 128] = block.T
+    right = lax.broadcasted_iota(jnp.int32, (64, 128), 1) >= 64
+    for i in range(5):
+        upper = packed_ref[UPPER[i] * 64 : UPPER[i] * 64 + 64, :]
+        lower = packed_ref[(25 + i // 2) * 64 : (26 + i // 2) * 64, :]
+        if i % 2:
+            lower = pltpu.roll(lower, 64, 1)
+        turned = jnp.concatenate([upper, upper]).T[64:]
+        square = slice(i * 128, (i + 1) * 128)
+        g_ref[square, square] = jnp.concatenate([upper, jnp.where(right, lower, turned)])
     t_ref[...] = start_ref[...]
     a_ref[...] = jnp.zeros_like(a_ref)
     for _ in range(ITERS):
@@ -259,7 +260,7 @@
 
 def shards(field, start):
     with jax.named_scope("regroup"):
-        pieces = regroup(field).reshape(16, 10, 40, 128)
+        pieces = field.transpose(1, 0, 2).reshape(16, 10, 40, 128)
         held = exchange(pieces, FIBRE)
     with jax.named_scope("gram"):
         core = lax.axis_index("c").astype(jnp.int32).reshape(1)
@@ -267,14 +268,13 @@
     with jax.named_scope("reduce_pair"):
         mine = parts[0] + lax.ppermute(parts[1], "c", SWAP)
     with jax.named_scope("reduce_plane"):
-        mine = exchange(mine.reshape(32, 32, 128), PLANE).sum(0)
+        mine = exchange(mine.reshape(32, 7, 4, 128), PLANE).sum(0)
     with jax.named_scope("sum_line"):
-        mine = exchange(jnp.broadcast_to(mine, (8, 32, 128)), "y").sum(0)
+        mine = exchange(jnp.broadcast_to(mine, (8, 7, 4, 128)), "y").sum(0)
     with jax.named_scope("gather_plane"):
-        mine = exchange(jnp.broadcast_to(mine, (32, 32, 128)), PLANE)
-        mine = mine.reshape(1024, 128)[:960]
+        mine = exchange(jnp.broadcast_to(mine, (32, 7, 4, 128)), PLANE)
     with jax.named_scope("gather_pair"):
-        packed = lax.all_gather(mine, "c", axis=0, tiled=True).reshape(15, 128, 128)
+        packed = lax.all_gather(mine.reshape(896, 128), "c", axis=0, tiled=True)
     with jax.named_scope("subspace"):
         basis, core = subspace_and_core(packed, start.T, high, low)
     return basis.T, core.transpose(1, 0, 2)

time: 183 us -> 181 us (0.989)
  local copies, waits for them, and re-layouts: 0.14 us -> 5.62 us
  Pallas kernels: 27.7 us -> 22.3 us
  blocking collectives: 65.6 us -> 62.7 us
    transpose x0 -> x1, local copies, waits for them, and re-layouts: none -> 5.51 us  [shards(): pieces = field.transpose(1, 0, 2).reshape(16, 10, 40, 128)]
    pallas_call x2 -> x1, Pallas kernels: 9.73 us -> 4.28 us  [local_gram(): pl.pallas_call(gram_kernel, out_shape=(jax.ShapeDtypeStruct((2, 896, 128)...]
    all_to_all x3, blocking collectives: 57.7 us -> 55.1 us  [exchange(): return lax.all_to_all(pieces, axes, 0, 0, tiled=True)]
where the time goes in v4:
time: 181 us; the launch traced here: 180 us
  waiting for transfers between devices  75.3 us (42%)
  blocking collectives  62.7 us (35%)
  Pallas kernels  22.3 us (12%)
  starting transfers between devices  13.3 us (7%)
  local copies, waits for them, and re-layouts  5.62 us (3%)
    all_to_all x1, waiting for transfers between devices, exchange(): return lax.all_to_all(pieces, axes, 0, 0, tiled=True)  73.9 us
    all_to_all x3, blocking collectives, exchange(): return lax.all_to_all(pieces, axes, 0, 0, tiled=True)  55.1 us
    pallas_call x1, Pallas kernels, subspace_and_core(): pl.pallas_call(subspace_kernel, out_shape=(jax.ShapeDtypeStruct((rank, ro...  18 us
    all_to_all x1, starting transfers between devices, exchange(): return lax.all_to_all(pieces, axes, 0, 0, tiled=True)  10.4 us
    all_gather x1, blocking collectives, shards(): packed = lax.all_gather(mine.reshape(896, 128), 'c', axis=0, tiled=True)  7.59 us
    transpose x1, local copies, waits for them, and re-layouts, shards(): pieces = field.transpose(1, 0, 2).reshape(16, 10, 40, 128)  5.51 us
    pallas_call x1, Pallas kernels, local_gram(): pl.pallas_call(gram_kernel, out_shape=(jax.ShapeDtypeStruct((2, 896, 128)...  4.28 us
  transfers between devices with their start and end apart: 2, of which 2 were waited for; matrix products, arithmetic and copies ran while one was open for 0% of the time, Pallas kernels for 0%

profile of v4, /device:TPU:1, one launch (start us, length us, event | category | flops | bytes accessed | tf_op | source)
XLA Modules:
  0.0 180.3 jit_solution(12416544285681311234)
XLA Ops:
  0.6 5.5 %copy.6 = f32[160,40,128]{2,1,0:T(8,128)} copy(f32[160,40,128]{2,0,1:T(8,128)} %bitcast.14) | data formatting | bytes 6553600 | tf_op jit(solution)/shard_map/regroup/transpose | solution.py:263
  6.1 10.4 %all-to-all-start = ((f32[16,10,40,128]{3,2,1,0:T(8,128)}), f32[16,10,40,128]{3,2,1,0:T(8,128)S(1)}, u32[]{:S(2)}, u32[]{:S(2)}) async-start(f32[16,10,40,128]{3,2,1,0:T(8,128)} %bitcast.13), calls=%async_computation | async-start | bytes 6553600 | tf_op jit(solution)/shard_map/regroup/all_to_all | solution.py:258
  16.5 73.9 %all-to-all-done.held_ref = f32[16,10,40,128]{3,2,1,0:T(8,128)S(1)} async-done(((f32[16,10,40,128]{3,2,1,0:T(8,128)}), f32[16,10,40,128]{3,2,1,0:T(8,128)S(1)}, u32[]{:S(2)}, u32[]{:S(2)}) %all-to-all-start) | async-done | bytes 3276832 | tf_op jit(solution)/shard_map/regroup/all_to_all | solution.py:258
  90.5 4.3 %gram.1 = (f32[2,896,128]{2,1,0:T(8,128)S(1)}, bf16[640,1280]{1,0:T(8,128)(2,1)}, bf16[640,1280]{1,0:T(8,128)(2,1)}) custom-call(s32[1]{0:T(128)} %bitcast.core_ref, f32[16,10,40,128]{3,2,1,0:T(8,128)S(1)} %all-to-all-done.held_ref), custom_call_target="tpu_custom_call" | custom-call | tf_op jit(solution)/shard_map/gram/pallas_call | solution.py:88
  94.8 0.0 copy-start
  94.8 2.9 %collective-permute-start = (f32[896,128]{1,0:T(8,128)S(1)}, f32[896,128]{1,0:T(8,128)S(1)}, u32[]{:S(2)}, u32[]{:S(2)}) collective-permute-start(f32[896,128]{1,0:T(8,128)S(1)} %slice_bitcast_fusion), channel_id=1, source_target_pairs={{0,32},{32,0},{1,33},{33,1},{2,34},{34,2},{3,35},{35,3},{4,36},{36... | collective-permute-start | bytes 1376264 | tf_op jit(solution)/shard_map/reduce_pair/ppermute | solution.py:269
  97.7 1.4 collective-permute-done
  99.2 26.3 %all_to_all.20 = f32[32,7,4,128]{3,2,1,0:T(4,128)S(1)} all-to-all(f32[32,7,4,128]{3,2,1,0:T(4,128)S(1)} %bitcast.15), channel_id=1, replica_groups=mesh['y'=8,'c'=2,'x'=4,'z'=8] {'z','x'}, dimensions={0} | all-to-all | bytes 917504 | tf_op jit(solution)/shard_map/reduce_plane/all_to_all | solution.py:258
  125.5 0.1 reduce_sum.18
  125.6 11.9 %all_to_all.21 = f32[8,7,4,128]{3,2,1,0:T(4,128)S(1)} all-to-all(f32[8,7,4,128]{3,2,1,0:T(4,128)S(1)} %broadcast_in_dim.6), channel_id=1, replica_groups=mesh['y'=8,'c'=2,'x'=4,'z'=8] {'y'}, dimensions={0} | all-to-all | bytes 229376 | tf_op jit(solution)/shard_map/sum_line/all_to_all | solution.py:258
  137.6 0.1 broadcast_in_dim.7
  137.6 16.9 %all_to_all.22 = f32[32,7,4,128]{3,2,1,0:T(4,128)S(1)} all-to-all(f32[32,7,4,128]{3,2,1,0:T(4,128)S(1)} %broadcast_in_dim.7), channel_id=1, replica_groups=mesh['y'=8,'c'=2,'x'=4,'z'=8] {'z','x'}, dimensions={0} | all-to-all | bytes 917504 | tf_op jit(solution)/shard_map/gather_plane/all_to_all | solution.py:258
  154.5 7.6 %all_gather.3.packed_ref = f32[1792,128]{1,0:T(8,128)S(1)} all-gather(f32[896,128]{1,0:T(8,128)S(1)} %bitcast.16), channel_id=1, replica_groups=mesh['y'=8,'c'=2,'x'=4,'z'=8] {'c'}, dimensions={0}, use_global_device_ids=true | all-gather | bytes 1376256 | tf_op jit(solution)/shard_map/gather_pair/all_gather | solution.py:277
  162.1 0.0 copy-done
  162.1 18.0 %subspace.1 = (f32[160,640]{1,0:T(8,128)}, f32[10,160,128]{2,1,0:T(8,128)}) custom-call(f32[1792,128]{1,0:T(8,128)S(1)} %all_gather.3.packed_ref, f32[160,640]{1,0:T(8,128)S(1)} %bitcast.12, bf16[640,1280]{1,0:T(8,128)(2,1)} %get-tuple-element.8.high_in, bf16[640,1280]{1,0:T(8,128)(2,1)} %get-tuple-element.9.low_in), custom_call_target="tpu_custom_call" | custom-call | tf_op jit(solution)/shard_map/subspace/pallas_call | solution.py:235
  (4 shorter events, 0.1 us)
Async XLA Ops:
  6.1 84.3 %all-to-all-start = ((f32[16,10,40,128]{3,2,1,0:T(8,128)}), f32[16,10,40,128]{3,2,1,0:T(8,128)S(1)}, u32[]{:S(2)}, u32[]{:S(2)}) async-start(f32[16,10,40,128]{3,2,1,0:T(8,128)} %bitcast.13), calls=%async_computation | async-start | bytes 6553600 | tf_op jit(solution)/shard_map/regroup/all_to_all | solution.py:258
  94.8 67.4 %copy-start = (f32[640,160]{0,1:T(8,128)S(1)}, f32[640,160]{0,1:T(8,128)}, u32[]{:S(2)}) copy-start(f32[640,160]{0,1:T(8,128)} %param.3) | copy-start | bytes 1228804
  94.8 4.3 %collective-permute-start = (f32[896,128]{1,0:T(8,128)S(1)}, f32[896,128]{1,0:T(8,128)S(1)}, u32[]{:S(2)}, u32[]{:S(2)}) collective-permute-start(f32[896,128]{1,0:T(8,128)S(1)} %slice_bitcast_fusion), channel_id=1, source_target_pairs={{0,32},{32,0},{1,33},{33,1},{2,34},{34,2},{3,35},{35,3},{4,36},{36... | collective-permute-start | bytes 1376264 | tf_op jit(solution)/shard_map/reduce_pair/ppermute | solution.py:269

commit v5 on v4

--- a/solution.py
+++ b/solution.py
@@ -42,6 +42,33 @@
 def halves(x):
     high = x.astype(BF)
     return high, (x - high.astype(F32)).astype(BF)
+
+
+def regroup_kernel(field_ref, out_ref, in_ref, sem):
+    parts = field_ref.shape[0] // 8
+    copies = []
+    for part in range(parts):
+        rows = pl.ds(8 * part, 8)
+        copies.append(
+            pltpu.make_async_copy(field_ref.at[rows], in_ref.at[rows], sem.at[part])
+        )
+        copies[-1].start()
+    for part, copy in enumerate(copies):
+        copy.wait()
+        rows = slice(8 * part, 8 * part + 8)
+        out_ref[:, rows, :] = jnp.swapaxes(in_ref[rows], 0, 1)
+
+
+def regroup(field):
+    rows, cells, lanes = field.shape
+    return pl.pallas_call(
+        regroup_kernel,
+        out_shape=jax.ShapeDtypeStruct((cells, rows, lanes), F32),
+        in_specs=[HBM],
+        out_specs=VMEM,
+        scratch_shapes=[pltpu.VMEM(field.shape, F32), pltpu.SemaphoreType.DMA((rows // 8,))],
+        compiler_params=BIG,
+    )(pltpu.with_memory_space_constraint(field, pltpu.HBM))
 
 
 def gram_kernel(core_ref, held_ref, out_ref, high_out, low_out, high_ref, low_ref, sem):
@@ -99,16 +126,23 @@
     )(core, held)
 
 
-def eliminate(square, w_ref):
+def eliminate(panel, w_ref):
     count = NB // 8
-    tiles = [square[8 * t : 8 * t + 8] for t in range(count)]
+    sides = range(len(panel))
+    tiles = [[side[8 * t : 8 * t + 8] for t in range(count)] for side in panel]
     for j in range(0, NB, STEP):
         t0 = j // 8
         cols = [
-            [jnp.broadcast_to(tiles[t][:, j + k : j + k + 1], (8, 128)) for t in range(t0, count)]
+            [
+                jnp.broadcast_to(tiles[0][t][:, j + k : j + k + 1], (8, 128))
+                for t in range(t0, count)
+            ]
             for k in range(STEP)
         ]
-        rows = [tiles[(j + k) // 8][(j + k) % 8 : (j + k) % 8 + 1, :] for k in range(STEP)]
+        rows = [
+            [tiles[s][(j + k) // 8][(j + k) % 8 : (j + k) % 8 + 1, :] for k in range(STEP)]
+            for s in sides
+        ]
         a = {
             (i, k): cols[k][(j + i) // 8 - t0][(j + i) % 8 : (j + i) % 8 + 1, :]
             for k in range(STEP)
@@ -116,24 +150,25 @@
         }
         for k in range(STEP):
             scale = lax.rsqrt(a[k, k])
-            rows[k] = rows[k] * scale
             for i in range(k + 1, STEP):
                 a[i, k] = a[i, k] * scale
             for i in range(k + 1, STEP):
                 for m in range(k + 1, i + 1):
                     a[i, m] = a[i, m] - a[i, k] * a[m, k]
-            for i in range(k + 1, STEP):
-                rows[i] = rows[i] - a[i, k] * rows[k]
+            for s in sides:
+                rows[s][k] = rows[s][k] * scale
+                for i in range(k + 1, STEP):
+                    rows[s][i] = rows[s][i] - a[i, k] * rows[s][k]
+                w_ref[j + k : j + k + 1, 128 * s : 128 * s + 128] = rows[s][k]
             cols[k] = [c * scale for c in cols[k]]
             for i in range(k + 1, STEP):
                 cols[i] = [c - a[i, k] * w for c, w in zip(cols[i], cols[k])]
-            w_ref[j + k : j + k + 1, :] = rows[k]
         for t in range((j + STEP) // 8, count):
-            change = cols[0][t - t0] * rows[0]
-            for k in range(1, STEP):
-                change = change + cols[k][t - t0] * rows[k]
-            tiles[t] = tiles[t] - change
-    return w_ref[:, NB : 2 * NB]
+            for s in sides:
+                change = cols[0][t - t0] * rows[s][0]
+                for k in range(1, STEP):
+                    change = change + cols[k][t - t0] * rows[s][k]
+                tiles[s][t] = tiles[s][t] - change
 
 
 def orthonormalize(a_ref, t_ref, w_ref):
@@ -143,25 +178,28 @@
     for k in range(rank // NB):
         own = slice(k * NB, (k + 1) * NB)
         rest = (k + 1) * NB
-        base = k * NB // 128 * 128
-        off = k * NB - base
-        block = a_ref[own, base : base + 128]
-        if off:
-            block = pltpu.roll(block, 128 - off, 1)
-        if off + NB > 128:
-            after = pltpu.roll(a_ref[own, base + 128 : base + 256], 128 - off, 1)
-            block = jnp.where(lane < 128 - off, block, after)
-        square = jnp.where(lane < NB, block, jnp.where(lane - NB == row, 1.0, 0.0))
-        w = eliminate(square, w_ref.at[k % 2])
+        n = rank - k * NB
+        w = w_ref.at[k % 2]
+        left = a_ref[own, :128]
+        if n + NB <= 128:
+            at = n
+            panel = [jnp.where(lane < n, left, jnp.where(lane - n == row, 1.0, 0.0))]
+        else:
+            at = max(n, 128)
+            right = jnp.where(lane - (at - 128) == row, 1.0, 0.0)
+            if n > 128:
+                right = jnp.where(lane < n - 128, a_ref[own, 128:], right)
+            panel = [left, right]
+        eliminate(panel, w)
+        inverse = w[:, at : at + NB]
         if rest < rank:
-            upper = dot(w, a_ref[own, :])
-            change = dot(upper[:, :rank], upper, TN)
-            a_ref[rest:, :] = a_ref[rest:, :] - change[rest:, :]
-        solved = dot(w, t_ref[own, :])
+            after = pltpu.roll(w[...], 256 - NB, 1)[:, :128]
+            moved = pltpu.roll(a_ref[rest:, :], 256 - NB, 1)[:, :128]
+            a_ref[rest:, :128] = moved - dot(after[:, : n - NB], after, TN)
+        solved = dot(inverse, t_ref[own, :])
         t_ref[own, :] = solved
         if rest < rank:
-            change = dot(upper[:, :rank], solved, TN)
-            t_ref[rest:, :] = t_ref[rest:, :] - change[rest:, :]
+            t_ref[rest:, :] = t_ref[rest:, :] - dot(after[:, : n - NB], solved, TN)
 
 
 def subspace_kernel(
@@ -244,7 +282,7 @@
             pltpu.VMEM((rows, rows), F32),
             pltpu.VMEM((rank, 256), F32),
             pltpu.VMEM((rank, rows), F32),
-            pltpu.VMEM((2, NB, 128), F32),
+            pltpu.VMEM((2, NB, 256), F32),
             pltpu.VMEM(high.shape, BF),
             pltpu.VMEM(low.shape, BF),
             pltpu.VMEM((cells, rank, 128), F32),
@@ -260,10 +298,11 @@
 
 def shards(field, start):
     with jax.named_scope("regroup"):
-        pieces = field.transpose(1, 0, 2).reshape(16, 10, 40, 128)
+        core = lax.axis_index("c").astype(jnp.int32).reshape(1)
+        pieces = regroup(field).reshape(16, 10, 40, 128)
+        pieces, core = lax.optimization_barrier((pieces, core))
         held = exchange(pieces, FIBRE)
     with jax.named_scope("gram"):
-        core = lax.axis_index("c").astype(jnp.int32).reshape(1)
         parts, high, low = local_gram(core, held)
     with jax.named_scope("reduce_pair"):
         mine = parts[0] + lax.ppermute(parts[1], "c", SWAP)

time: 181 us -> 175 us (0.967)
  blocking collectives: 62.7 us -> 148 us
  waiting for transfers between devices: 75.3 us -> 1.78 us
  starting transfers between devices: 13.3 us -> 2.05 us
  local copies, waits for them, and re-layouts: 5.62 us -> 0.12 us
    all_to_all x3 -> x4, blocking collectives: 55.1 us -> 140 us  [exchange(): return lax.all_to_all(pieces, axes, 0, 0, tiled=True)]
    all_to_all x1 -> x0, waiting for transfers between devices: 73.9 us -> none  [exchange(): return lax.all_to_all(pieces, axes, 0, 0, tiled=True)]
    all_to_all x1 -> x0, starting transfers between devices: 10.4 us -> none  [exchange(): return lax.all_to_all(pieces, axes, 0, 0, tiled=True)]
    transpose x1 -> x0, local copies, waits for them, and re-layouts: 5.51 us -> none  [shards(): pieces = field.transpose(1, 0, 2).reshape(16, 10, 40, 128)]
    pallas_call x1, Pallas kernels: 18 us -> 15.8 us  [subspace_and_core(): pl.pallas_call(subspace_kernel, out_shape=(jax.ShapeDtypeStruct((rank, ro...]
    pallas_call x0 -> x1, Pallas kernels: none -> 2.04 us  [regroup(): pl.pallas_call(regroup_kernel, out_shape=jax.ShapeDtypeStruct((cells, row...]
  transfers between devices with their start and end apart: 2 -> 1, of which waited for: 2 -> 1; matrix products, arithmetic and copies ran while one was open for 0% -> 0% of each run, Pallas kernels for 0% -> 0%
where the time goes in v5:
time: 175 us
  blocking collectives  148 us (85%)
  Pallas kernels  22.3 us (13%)
  starting transfers between devices  2.05 us (1%)
  waiting for transfers between devices  1.78 us (1%)
    all_to_all x4, blocking collectives, exchange(): return lax.all_to_all(pieces, axes, 0, 0, tiled=True)  140 us
    pallas_call x1, Pallas kernels, subspace_and_core(): pl.pallas_call(subspace_kernel, out_shape=(jax.ShapeDtypeStruct((rank, ro...  15.8 us
    all_gather x1, blocking collectives, shards(): packed = lax.all_gather(mine.reshape(896, 128), 'c', axis=0, tiled=True)  7.48 us
    pallas_call x1, Pallas kernels, local_gram(): pl.pallas_call(gram_kernel, out_shape=(jax.ShapeDtypeStruct((2, 896, 128)...  4.39 us
  transfers between devices with their start and end apart: 1, of which 1 were waited for; matrix products, arithmetic and copies ran while one was open for 0% of the time, Pallas kernels for 0%

profile of v5, /device:TPU:1, one launch (start us, length us, event | category | flops | bytes accessed | tf_op | source)
XLA Modules:
  0.0 174.9 jit_solution(1822178961842569789)
XLA Ops:
  0.6 2.0 %regroup.1 = f32[160,40,128]{2,1,0:T(8,128)S(1)} custom-call(f32[40,160,128]{2,1,0:T(8,128)} %field_ref.1), custom_call_target="tpu_custom_call" | custom-call | tf_op jit(solution)/shard_map/regroup/pallas_call | solution.py:64
  2.7 85.9 %all_to_all.20.held_ref = f32[16,10,40,128]{3,2,1,0:T(8,128)S(1)} all-to-all(f32[16,10,40,128]{3,2,1,0:T(8,128)S(1)} %bitcast.11), channel_id=1, replica_groups=mesh['y'=8,'c'=2,'x'=4,'z'=8] {'y','c'}, dimensions={0} | all-to-all | bytes 6553600 | tf_op jit(solution)/shard_map/regroup/all_to_all | solution.py:296
  88.6 4.4 %gram.1 = (f32[2,896,128]{2,1,0:T(8,128)S(1)}, bf16[640,1280]{1,0:T(8,128)(2,1)}, bf16[640,1280]{1,0:T(8,128)(2,1)}) custom-call(s32[1]{0:T(128)} %bitcast.1.core_ref, f32[16,10,40,128]{3,2,1,0:T(8,128)S(1)} %all_to_all.20.held_ref), custom_call_target="tpu_custom_call" | custom-call | tf_op jit(solution)/shard_map/gram/pallas_call | solution.py:115
  93.0 0.0 copy-start
  93.0 2.1 %collective-permute-start = (f32[896,128]{1,0:T(8,128)S(1)}, f32[896,128]{1,0:T(8,128)S(1)}, u32[]{:S(2)}, u32[]{:S(2)}) collective-permute-start(f32[896,128]{1,0:T(8,128)S(1)} %slice_bitcast_fusion), channel_id=1, source_target_pairs={{0,32},{32,0},{1,33},{33,1},{2,34},{34,2},{3,35},{35,3},{4,36},{36... | collective-permute-start | bytes 1376264 | tf_op jit(solution)/shard_map/reduce_pair/ppermute | solution.py:308
  95.1 1.8 %collective-permute-done = f32[896,128]{1,0:T(8,128)S(1)} collective-permute-done((f32[896,128]{1,0:T(8,128)S(1)}, f32[896,128]{1,0:T(8,128)S(1)}, u32[]{:S(2)}, u32[]{:S(2)}) %collective-permute-start) | collective-permute-done | bytes 458784 | tf_op jit(solution)/shard_map/reduce_pair/ppermute | solution.py:308
  96.9 27.1 %all_to_all.21 = f32[32,7,4,128]{3,2,1,0:T(4,128)S(1)} all-to-all(f32[32,7,4,128]{3,2,1,0:T(4,128)S(1)} %bitcast.13), channel_id=1, replica_groups=mesh['y'=8,'c'=2,'x'=4,'z'=8] {'z','x'}, dimensions={0} | all-to-all | bytes 917504 | tf_op jit(solution)/shard_map/reduce_plane/all_to_all | solution.py:296
  124.0 0.1 reduce_sum.18
  124.1 10.2 %all_to_all.22 = f32[8,7,4,128]{3,2,1,0:T(4,128)S(1)} all-to-all(f32[8,7,4,128]{3,2,1,0:T(4,128)S(1)} %broadcast_in_dim.6), channel_id=1, replica_groups=mesh['y'=8,'c'=2,'x'=4,'z'=8] {'y'}, dimensions={0} | all-to-all | bytes 229376 | tf_op jit(solution)/shard_map/sum_line/all_to_all | solution.py:296
  134.4 0.1 broadcast_in_dim.7
  134.5 16.9 %all_to_all.23 = f32[32,7,4,128]{3,2,1,0:T(4,128)S(1)} all-to-all(f32[32,7,4,128]{3,2,1,0:T(4,128)S(1)} %broadcast_in_dim.7), channel_id=1, replica_groups=mesh['y'=8,'c'=2,'x'=4,'z'=8] {'z','x'}, dimensions={0} | all-to-all | bytes 917504 | tf_op jit(solution)/shard_map/gather_plane/all_to_all | solution.py:296
  151.4 7.5 %all_gather.3.packed_ref = f32[1792,128]{1,0:T(8,128)S(1)} all-gather(f32[896,128]{1,0:T(8,128)S(1)} %bitcast.14), channel_id=1, replica_groups=mesh['y'=8,'c'=2,'x'=4,'z'=8] {'c'}, dimensions={0}, use_global_device_ids=true | all-gather | bytes 1376256 | tf_op jit(solution)/shard_map/gather_pair/all_gather | solution.py:316
  158.9 0.0 copy-done
  158.9 15.8 %subspace.1 = (f32[160,640]{1,0:T(8,128)}, f32[10,160,128]{2,1,0:T(8,128)}) custom-call(f32[1792,128]{1,0:T(8,128)S(1)} %all_gather.3.packed_ref, f32[160,640]{1,0:T(8,128)S(1)} %bitcast.12, bf16[640,1280]{1,0:T(8,128)(2,1)} %get-tuple-element.12.high_in, bf16[640,1280]{1,0:T(8,128)(2,1)} %get-tuple-element.13.low_in), custom_call_target="tpu_custom_call" | custom-call | tf_op jit(solution)/shard_map/subspace/pallas_call | solution.py:273
  (4 shorter events, 0.1 us)
Async XLA Ops:
  93.0 65.9 %copy-start = (f32[640,160]{0,1:T(8,128)S(1)}, f32[640,160]{0,1:T(8,128)}, u32[]{:S(2)}) copy-start(f32[640,160]{0,1:T(8,128)} %param.3) | copy-start | bytes 1228804
  93.0 3.8 %collective-permute-start = (f32[896,128]{1,0:T(8,128)S(1)}, f32[896,128]{1,0:T(8,128)S(1)}, u32[]{:S(2)}, u32[]{:S(2)}) collective-permute-start(f32[896,128]{1,0:T(8,128)S(1)} %slice_bitcast_fusion), channel_id=1, source_target_pairs={{0,32},{32,0},{1,33},{33,1},{2,34},{34,2},{3,35},{35,3},{4,36},{36... | collective-permute-start | bytes 1376264 | tf_op jit(solution)/shard_map/reduce_pair/ppermute | solution.py:308

commit v6 on v5

--- a/solution.py
+++ b/solution.py
@@ -9,9 +9,9 @@
 
 ITERS = 2
 FIBRE = ("y", "c")
-PLANE = ("z", "x")
+PLANE = ("x", "z")
 SWAP = [(0, 1), (1, 0)]
-NB = 40
+NB = 80
 STEP = 8
 UPPER = [20, 21, 22, 23, 24]
 ACROSS = {
@@ -72,15 +72,22 @@
 
 
 def gram_kernel(core_ref, held_ref, out_ref, high_out, low_out, high_ref, low_ref, sem):
-    for p in range(held_ref.shape[1]):
-        x = held_ref[:, p].reshape(640, 128)
-        high_ref[:, p * 128 : (p + 1) * 128], low_ref[:, p * 128 : (p + 1) * 128] = halves(x)
-    copies = [
-        pltpu.make_async_copy(high_ref, high_out, sem.at[0]),
-        pltpu.make_async_copy(low_ref, low_out, sem.at[1]),
-    ]
-    for copy in copies:
-        copy.start()
+    cells = held_ref.shape[1]
+    copies = []
+    for group in range(2):
+        first, last = group * cells // 2, (group + 1) * cells // 2
+        for p in range(first, last):
+            x = held_ref[:, p].reshape(640, 128)
+            lanes = slice(p * 128, (p + 1) * 128)
+            high_ref[:, lanes], low_ref[:, lanes] = halves(x)
+        lanes = pl.ds(first * 128, (last - first) * 128)
+        for at, (source, target) in enumerate(((high_ref, high_out), (low_ref, low_out))):
+            copies.append(
+                pltpu.make_async_copy(
+                    source.at[:, lanes], target.at[:, lanes], sem.at[2 * group + at]
+                )
+            )
+            copies[-1].start()
     core = core_ref[0]
 
     def put(strip, value):
@@ -120,7 +127,7 @@
         scratch_shapes=[
             pltpu.VMEM(flat.shape, BF),
             pltpu.VMEM(flat.shape, BF),
-            pltpu.SemaphoreType.DMA((2,)),
+            pltpu.SemaphoreType.DMA((4,)),
         ],
         compiler_params=BIG,
     )(core, held)

time: 175 us -> 173 us (0.989)
  no operation moved by 1% of the time
where the time goes in v6:
time: 173 us
  blocking collectives  147 us (85%)
  Pallas kernels  20.8 us (12%)
  starting transfers between devices  2.05 us (1%)
  waiting for transfers between devices  1.78 us (1%)
    all_to_all x4, blocking collectives, exchange(): return lax.all_to_all(pieces, axes, 0, 0, tiled=True)  140 us
    pallas_call x1, Pallas kernels, subspace_and_core(): pl.pallas_call(subspace_kernel, out_shape=(jax.ShapeDtypeStruct((rank, ro...  15.1 us
    all_gather x1, blocking collectives, shards(): packed = lax.all_gather(mine.reshape(896, 128), 'c', axis=0, tiled=True)  7.42 us
    pallas_call x1, Pallas kernels, local_gram(): pl.pallas_call(gram_kernel, out_shape=(jax.ShapeDtypeStruct((2, 896, 128)...  3.66 us
  transfers between devices with their start and end apart: 1, of which 1 were waited for; matrix products, arithmetic and copies ran while one was open for 0% of the time, Pallas kernels for 0%

profile of v6, /device:TPU:1, one launch (start us, length us, event | category | flops | bytes accessed | tf_op | source)
XLA Modules:
  0.0 172.7 jit_solution(12297821464427133055)
XLA Ops:
  0.6 2.0 %regroup.1 = f32[160,40,128]{2,1,0:T(8,128)S(1)} custom-call(f32[40,160,128]{2,1,0:T(8,128)} %field_ref.1), custom_call_target="tpu_custom_call" | custom-call | tf_op jit(solution)/shard_map/regroup/pallas_call | solution.py:64
  2.7 85.9 %all_to_all.20.held_ref = f32[16,10,40,128]{3,2,1,0:T(8,128)S(1)} all-to-all(f32[16,10,40,128]{3,2,1,0:T(8,128)S(1)} %bitcast.11), channel_id=1, replica_groups=mesh['y'=8,'c'=2,'x'=4,'z'=8] {'y','c'}, dimensions={0} | all-to-all | bytes 6553600 | tf_op jit(solution)/shard_map/regroup/all_to_all | solution.py:303
  88.6 3.7 %gram.1 = (f32[2,896,128]{2,1,0:T(8,128)S(1)}, bf16[640,1280]{1,0:T(8,128)(2,1)}, bf16[640,1280]{1,0:T(8,128)(2,1)}) custom-call(s32[1]{0:T(128)} %bitcast.1.core_ref, f32[16,10,40,128]{3,2,1,0:T(8,128)S(1)} %all_to_all.20.held_ref), custom_call_target="tpu_custom_call" | custom-call | tf_op jit(solution)/shard_map/gram/pallas_call | solution.py:122
  92.2 0.0 copy-start
  92.3 2.1 %collective-permute-start = (f32[896,128]{1,0:T(8,128)S(1)}, f32[896,128]{1,0:T(8,128)S(1)}, u32[]{:S(2)}, u32[]{:S(2)}) collective-permute-start(f32[896,128]{1,0:T(8,128)S(1)} %slice_bitcast_fusion), channel_id=1, source_target_pairs={{0,32},{32,0},{1,33},{33,1},{2,34},{34,2},{3,35},{35,3},{4,36},{36... | collective-permute-start | bytes 1376264 | tf_op jit(solution)/shard_map/reduce_pair/ppermute | solution.py:315
  94.3 1.8 %collective-permute-done = f32[896,128]{1,0:T(8,128)S(1)} collective-permute-done((f32[896,128]{1,0:T(8,128)S(1)}, f32[896,128]{1,0:T(8,128)S(1)}, u32[]{:S(2)}, u32[]{:S(2)}) %collective-permute-start) | collective-permute-done | bytes 458784 | tf_op jit(solution)/shard_map/reduce_pair/ppermute | solution.py:315
  96.2 24.7 %all_to_all.21 = f32[32,7,4,128]{3,2,1,0:T(4,128)S(1)} all-to-all(f32[32,7,4,128]{3,2,1,0:T(4,128)S(1)} %bitcast.13), channel_id=1, replica_groups=mesh['y'=8,'c'=2,'x'=4,'z'=8] {'x','z'}, dimensions={0} | all-to-all | bytes 917504 | tf_op jit(solution)/shard_map/reduce_plane/all_to_all | solution.py:303
  120.9 0.1 reduce_sum.18
  121.0 10.1 %all_to_all.22 = f32[8,7,4,128]{3,2,1,0:T(4,128)S(1)} all-to-all(f32[8,7,4,128]{3,2,1,0:T(4,128)S(1)} %broadcast_in_dim.6), channel_id=1, replica_groups=mesh['y'=8,'c'=2,'x'=4,'z'=8] {'y'}, dimensions={0} | all-to-all | bytes 229376 | tf_op jit(solution)/shard_map/sum_line/all_to_all | solution.py:303
  131.2 0.1 broadcast_in_dim.7
  131.2 18.8 %all_to_all.23 = f32[32,7,4,128]{3,2,1,0:T(4,128)S(1)} all-to-all(f32[32,7,4,128]{3,2,1,0:T(4,128)S(1)} %broadcast_in_dim.7), channel_id=1, replica_groups=mesh['y'=8,'c'=2,'x'=4,'z'=8] {'x','z'}, dimensions={0} | all-to-all | bytes 917504 | tf_op jit(solution)/shard_map/gather_plane/all_to_all | solution.py:303
  150.1 7.4 %all_gather.3.packed_ref = f32[1792,128]{1,0:T(8,128)S(1)} all-gather(f32[896,128]{1,0:T(8,128)S(1)} %bitcast.14), channel_id=1, replica_groups=mesh['y'=8,'c'=2,'x'=4,'z'=8] {'c'}, dimensions={0}, use_global_device_ids=true | all-gather | bytes 1376256 | tf_op jit(solution)/shard_map/gather_pair/all_gather | solution.py:323
  157.5 0.0 copy-done
  157.5 15.1 %subspace.1 = (f32[160,640]{1,0:T(8,128)}, f32[10,160,128]{2,1,0:T(8,128)}) custom-call(f32[1792,128]{1,0:T(8,128)S(1)} %all_gather.3.packed_ref, f32[160,640]{1,0:T(8,128)S(1)} %bitcast.12, bf16[640,1280]{1,0:T(8,128)(2,1)} %get-tuple-element.12.high_in, bf16[640,1280]{1,0:T(8,128)(2,1)} %get-tuple-element.13.low_in), custom_call_target="tpu_custom_call" | custom-call | tf_op jit(solution)/shard_map/subspace/pallas_call | solution.py:280
  (4 shorter events, 0.1 us)
Async XLA Ops:
  92.2 65.2 %copy-start = (f32[640,160]{0,1:T(8,128)S(1)}, f32[640,160]{0,1:T(8,128)}, u32[]{:S(2)}) copy-start(f32[640,160]{0,1:T(8,128)} %param.3) | copy-start | bytes 1228804
  92.3 3.8 %collective-permute-start = (f32[896,128]{1,0:T(8,128)S(1)}, f32[896,128]{1,0:T(8,128)S(1)}, u32[]{:S(2)}, u32[]{:S(2)}) collective-permute-start(f32[896,128]{1,0:T(8,128)S(1)} %slice_bitcast_fusion), channel_id=1, source_target_pairs={{0,32},{32,0},{1,33},{33,1},{2,34},{34,2},{3,35},{35,3},{4,36},{36... | collective-permute-start | bytes 1376264 | tf_op jit(solution)/shard_map/reduce_pair/ppermute | solution.py:315

commit v7 on v6

--- a/solution.py
+++ b/solution.py
@@ -9,7 +9,9 @@
 
 ITERS = 2
 FIBRE = ("y", "c")
-PLANE = ("x", "z")
+SENT = ("c", "y")
+PLACE = [f % 2 * 8 + f // 2 for f in range(16)]
+PLANE = ("z", "x")
 SWAP = [(0, 1), (1, 0)]
 NB = 80
 STEP = 8
@@ -56,7 +58,12 @@
     for part, copy in enumerate(copies):
         copy.wait()
         rows = slice(8 * part, 8 * part + 8)
-        out_ref[:, rows, :] = jnp.swapaxes(in_ref[rows], 0, 1)
+        turned = jnp.swapaxes(in_ref[rows], 0, 1)
+        each = turned.shape[0] // 16
+        for f, place in enumerate(PLACE):
+            out_ref[place * each : (place + 1) * each, rows, :] = turned[
+                f * each : (f + 1) * each
+            ]
 
 
 def regroup(field):
@@ -77,7 +84,7 @@
     for group in range(2):
         first, last = group * cells // 2, (group + 1) * cells // 2
         for p in range(first, last):
-            x = held_ref[:, p].reshape(640, 128)
+            x = jnp.concatenate([held_ref[place, p] for place in PLACE])
             lanes = slice(p * 128, (p + 1) * 128)
             high_ref[:, lanes], low_ref[:, lanes] = halves(x)
         lanes = pl.ds(first * 128, (last - first) * 128)
@@ -308,7 +315,7 @@
         core = lax.axis_index("c").astype(jnp.int32).reshape(1)
         pieces = regroup(field).reshape(16, 10, 40, 128)
         pieces, core = lax.optimization_barrier((pieces, core))
-        held = exchange(pieces, FIBRE)
+        held = exchange(pieces, SENT)
     with jax.named_scope("gram"):
         parts, high, low = local_gram(core, held)
     with jax.named_scope("reduce_pair"):

time: 173 us -> 173 us (level)
  no operation moved by 1% of the time
where the time goes in v7:
time: 173 us
  blocking collectives  146 us (84%)
  Pallas kernels  20.8 us (12%)
  starting transfers between devices  3.3 us (2%)
    all_to_all x4, blocking collectives, exchange(): return lax.all_to_all(pieces, axes, 0, 0, tiled=True)  139 us
    pallas_call x1, Pallas kernels, subspace_and_core(): pl.pallas_call(subspace_kernel, out_shape=(jax.ShapeDtypeStruct((rank, ro...  15.1 us
    all_gather x1, blocking collectives, shards(): packed = lax.all_gather(mine.reshape(896, 128), 'c', axis=0, tiled=True)  7.59 us
    pallas_call x1, Pallas kernels, local_gram(): pl.pallas_call(gram_kernel, out_shape=(jax.ShapeDtypeStruct((2, 896, 128)...  3.66 us
  transfers between devices with their start and end apart: 1, of which 1 were waited for; matrix products, arithmetic and copies ran while one was open for 0% of the time, Pallas kernels for 0%

profile of v7, /device:TPU:1, one launch (start us, length us, event | category | flops | bytes accessed | tf_op | source)
XLA Modules:
  0.0 173.0 jit_solution(2025986735872493462)
XLA Ops:
  0.6 2.0 %regroup.1 = f32[160,40,128]{2,1,0:T(8,128)S(1)} custom-call(f32[40,160,128]{2,1,0:T(8,128)} %field_ref.1), custom_call_target="tpu_custom_call" | custom-call | tf_op jit(solution)/shard_map/regroup/pallas_call | solution.py:71
  2.7 84.2 %all_to_all.20.held_ref = f32[16,10,40,128]{3,2,1,0:T(8,128)S(1)} all-to-all(f32[16,10,40,128]{3,2,1,0:T(8,128)S(1)} %bitcast.11), channel_id=1, replica_groups=mesh['y'=8,'c'=2,'x'=4,'z'=8] {'c','y'}, dimensions={0} | all-to-all | bytes 6553600 | tf_op jit(solution)/shard_map/regroup/all_to_all | solution.py:310
  86.9 3.7 %gram.1 = (f32[2,896,128]{2,1,0:T(8,128)S(1)}, bf16[640,1280]{1,0:T(8,128)(2,1)}, bf16[640,1280]{1,0:T(8,128)(2,1)}) custom-call(s32[1]{0:T(128)} %bitcast.1.core_ref, f32[16,10,40,128]{3,2,1,0:T(8,128)S(1)} %all_to_all.20.held_ref), custom_call_target="tpu_custom_call" | custom-call | tf_op jit(solution)/shard_map/gram/pallas_call | solution.py:129
  90.6 0.0 copy-start
  90.6 3.3 %collective-permute-start = (f32[896,128]{1,0:T(8,128)S(1)}, f32[896,128]{1,0:T(8,128)S(1)}, u32[]{:S(2)}, u32[]{:S(2)}) collective-permute-start(f32[896,128]{1,0:T(8,128)S(1)} %slice_bitcast_fusion), channel_id=1, source_target_pairs={{0,32},{32,0},{1,33},{33,1},{2,34},{34,2},{3,35},{35,3},{4,36},{36... | collective-permute-start | bytes 1376264 | tf_op jit(solution)/shard_map/reduce_pair/ppermute | solution.py:322
  93.9 1.4 collective-permute-done
  95.4 27.4 %all_to_all.21 = f32[32,7,4,128]{3,2,1,0:T(4,128)S(1)} all-to-all(f32[32,7,4,128]{3,2,1,0:T(4,128)S(1)} %bitcast.13), channel_id=1, replica_groups=mesh['y'=8,'c'=2,'x'=4,'z'=8] {'z','x'}, dimensions={0} | all-to-all | bytes 917504 | tf_op jit(solution)/shard_map/reduce_plane/all_to_all | solution.py:310
  122.8 0.1 reduce_sum.18
  122.9 10.3 %all_to_all.22 = f32[8,7,4,128]{3,2,1,0:T(4,128)S(1)} all-to-all(f32[8,7,4,128]{3,2,1,0:T(4,128)S(1)} %broadcast_in_dim.6), channel_id=1, replica_groups=mesh['y'=8,'c'=2,'x'=4,'z'=8] {'y'}, dimensions={0} | all-to-all | bytes 229376 | tf_op jit(solution)/shard_map/sum_line/all_to_all | solution.py:310
  133.2 0.1 broadcast_in_dim.7
  133.3 16.9 %all_to_all.23 = f32[32,7,4,128]{3,2,1,0:T(4,128)S(1)} all-to-all(f32[32,7,4,128]{3,2,1,0:T(4,128)S(1)} %broadcast_in_dim.7), channel_id=1, replica_groups=mesh['y'=8,'c'=2,'x'=4,'z'=8] {'z','x'}, dimensions={0} | all-to-all | bytes 917504 | tf_op jit(solution)/shard_map/gather_plane/all_to_all | solution.py:310
  150.2 7.6 %all_gather.3.packed_ref = f32[1792,128]{1,0:T(8,128)S(1)} all-gather(f32[896,128]{1,0:T(8,128)S(1)} %bitcast.14), channel_id=1, replica_groups=mesh['y'=8,'c'=2,'x'=4,'z'=8] {'c'}, dimensions={0}, use_global_device_ids=true | all-gather | bytes 1376256 | tf_op jit(solution)/shard_map/gather_pair/all_gather | solution.py:330
  157.8 0.0 copy-done
  157.8 15.1 %subspace.1 = (f32[160,640]{1,0:T(8,128)}, f32[10,160,128]{2,1,0:T(8,128)}) custom-call(f32[1792,128]{1,0:T(8,128)S(1)} %all_gather.3.packed_ref, f32[160,640]{1,0:T(8,128)S(1)} %bitcast.12, bf16[640,1280]{1,0:T(8,128)(2,1)} %get-tuple-element.12.high_in, bf16[640,1280]{1,0:T(8,128)(2,1)} %get-tuple-element.13.low_in), custom_call_target="tpu_custom_call" | custom-call | tf_op jit(solution)/shard_map/subspace/pallas_call | solution.py:287
  (4 shorter events, 0.1 us)
Async XLA Ops:
  90.6 67.2 %copy-start = (f32[640,160]{0,1:T(8,128)S(1)}, f32[640,160]{0,1:T(8,128)}, u32[]{:S(2)}) copy-start(f32[640,160]{0,1:T(8,128)} %param.3) | copy-start | bytes 1228804
  90.6 4.7 %collective-permute-start = (f32[896,128]{1,0:T(8,128)S(1)}, f32[896,128]{1,0:T(8,128)S(1)}, u32[]{:S(2)}, u32[]{:S(2)}) collective-permute-start(f32[896,128]{1,0:T(8,128)S(1)} %slice_bitcast_fusion), channel_id=1, source_target_pairs={{0,32},{32,0},{1,33},{33,1},{2,34},{34,2},{3,35},{35,3},{4,36},{36... | collective-permute-start | bytes 1376264 | tf_op jit(solution)/shard_map/reduce_pair/ppermute | solution.py:322
